TPU v7x, 256 devices: a whole 4x4x8 slice. The times are simulated.
256 devices in a mesh: chan: 32 (over x, y, core), wide: 8 (over z).
Axes of the slice: x: 4, y: 4, z: 8, core: 2. Of those that a mesh axis runs over, the one named last changes fastest.
Arguments:
- conc_now: float32 [8, 64, 64, 1024], P(None, 'chan', None, 'wide'), may hold values from 0.01 to 1
- conc_prev: float32 [8, 64, 64, 1024], P(None, 'chan', None, 'wide'), may hold values from 0.1 to 1
- phi_prev: float32 [64, 64, 1024], P('chan', None, 'wide'), may hold values from -3 to 3
- owner: int32 [64, 64, 1024], P('chan', None, 'wide'), may hold values from 0 to 2048, as said below
- partner: int32 [2048], replicated, may hold values from 0 to 2047, each once
- valence: int32 [8], replicated, may hold values from -2 to 2
- diffusivity: float32 [8], replicated, may hold values from 0.2 to 1
Outputs:
- conc_next: float32 [8, 64, 64, 1024], P(None, 'chan', None, 'wide')
- potential: float32 [64, 64, 1024], P('chan', None, 'wide')
Inputs may be any that keep to these rules, and one draw needn't show every extreme that they name: `owner`: the value 2048 marks a cell of no junction. The cells of one junction lie within one block of 2 cells along the length and 128 along the width, aligned with the grid. Some junctions own no cell. `partner`: every junction appears once.
All inputs are finite; a program needn't handle non-finite values.
Results may differ from a plain program's by a relative error of at most 0.00029.
Values sent between devices are 32-bit elements; how exact they have to be, the bound alone decides.
A program may use at most 128 MiB of HBM per device.

v0:
```python
import math

import jax
import jax.numpy as jnp
from jax import lax
from jax.sharding import PartitionSpec as P

SWEEPS = 4


time_step = 0.5
coupling = 2.0
charge_scale = 0.05
conduct_ref = 1.5
highest = lax.Precision.HIGHEST


def with_halo(cells, sides, width):
    for axis, dim in sides:
        count = lax.axis_size(axis)
        ends = count - 1
        head = lax.slice_in_dim(cells, 0, width, axis=dim)
        tail = lax.slice_in_dim(cells, cells.shape[dim] - width, cells.shape[dim], axis=dim)
        cells = jnp.concatenate(
            [
                lax.ppermute(tail, axis, [(i, (i + 1) % count) for i in range(ends)]),
                cells,
                lax.ppermute(head, axis, [((i + 1) % count, i) for i in range(ends)]),
            ],
            axis=dim,
        )
    return cells


def sine_table(length):
    index = jnp.arange(length).astype(jnp.float32) + 1.0
    return math.sqrt(2.0 / (length + 1.0)) * jnp.sin(
        math.pi * index[:, None] * index[None, :] / (length + 1.0)
    )


def eigen_values(length):
    index = jnp.arange(length).astype(jnp.float32) + 1.0
    return 2.0 - 2.0 * jnp.cos(math.pi * index / (length + 1.0))


def conductivity(concs, valence, diffusivity):
    charge_sq = (valence * valence).astype(jnp.float32)
    weights = charge_sq * diffusivity / jnp.sum((charge_sq + 1.0) * diffusivity)
    return 1.0 + jnp.sum(weights[:, None, None, None] * concs * concs, axis=0)


def neighbours(padded, depth_mode):
    middle = padded[..., 1:-1, :, 1:-1]
    widths = [(0, 0)] * (padded.ndim - 3) + [(0, 0), (1, 1), (0, 0)]
    depth_padded = jnp.pad(middle, widths, mode=depth_mode)
    return [
        padded[..., :-2, :, 1:-1],
        padded[..., 2:, :, 1:-1],
        depth_padded[..., :-2, :],
        depth_padded[..., 2:, :],
        padded[..., 1:-1, :, :-2],
        padded[..., 1:-1, :, 2:],
    ]


def rim_replace(padded, lower_x, upper_x, lower_y, upper_y):
    low_plane = jnp.where(lower_x, padded[..., 1:2, :, :], padded[..., 0:1, :, :])
    high_plane = jnp.where(upper_x, padded[..., -2:-1, :, :], padded[..., -1:, :, :])
    padded = jnp.concatenate([low_plane, padded[..., 1:-1, :, :], high_plane], axis=-3)
    low_plane = jnp.where(lower_y, padded[..., 1:2], padded[..., 0:1])
    high_plane = jnp.where(upper_y, padded[..., -2:-1], padded[..., -1:])
    return jnp.concatenate([low_plane, padded[..., 1:-1], high_plane], axis=-1)


def halo_potential(potential_field):
    return with_halo(potential_field, (("chan", 0), ("wide", 2)), 1)


def per_device(conc_now, conc_prev, phi_prev, owner, partner, valence, diffusivity):
    species_all, cells_x, depth_all, cells_y = conc_now.shape
    chan_total = lax.axis_size("chan")
    wide_total = lax.axis_size("wide")
    chan_place = lax.axis_index("chan")
    wide_place = lax.axis_index("wide")
    length_all = cells_x * chan_total
    width_all = cells_y * wide_total
    depth_piece = depth_all // wide_total
    width_piece = width_all // chan_total
    junction_total = partner.shape[0]
    lower_x = chan_place == 0
    upper_x = chan_place == chan_total - 1
    lower_y = wide_place == 0
    upper_y = wide_place == wide_total - 1
    table_x = sine_table(length_all)
    table_z = sine_table(depth_all)
    table_y = sine_table(width_all)
    eigen_x = eigen_values(length_all)
    eigen_y = eigen_values(width_all)
    eigen_z = lax.dynamic_slice_in_dim(
        eigen_values(depth_all), wide_place * depth_piece, depth_piece
    )
    charge_weights = valence.astype(jnp.float32)[:, None, None, None]
    drift = (valence.astype(jnp.float32) * diffusivity)[:, None, None, None]
    spread = diffusivity[:, None, None, None]
    owners = jnp.minimum(owner.reshape(-1), junction_total)
    cell_counts = jax.ops.segment_sum(
        jnp.ones(owners.shape, jnp.float32), owners, num_segments=junction_total + 1
    )
    concs = conc_now
    potential_field = phi_prev
    conc_raw = with_halo(concs, (("chan", 1), ("wide", 3)), 1)
    sigma_local = conductivity(concs, valence, diffusivity)
    sigma_padded = with_halo(sigma_local, (("chan", 0), ("wide", 2)), 1)
    charge = charge_scale * jnp.sum(charge_weights * concs, axis=0)
    for sweep_step in range(SWEEPS):
        phi_padded = halo_potential(potential_field)
        apply_phi_near_all = neighbours(phi_padded, "constant")
        sigma_near_all = neighbours(sigma_padded, "constant")
        sigma_mid = sigma_padded[1:-1, :, 1:-1]
        applied = jnp.zeros_like(potential_field)
        for apply_phi_near, sigma_near in zip(apply_phi_near_all, sigma_near_all):
            applied = applied + 0.5 * (sigma_mid + sigma_near) * (potential_field - apply_phi_near)
        spectrum = jnp.einsum("az,xzy->xay", table_z, charge - applied, precision=highest)
        spectrum = lax.all_to_all(spectrum, "wide", split_axis=1, concat_axis=2, tiled=True)
        across = jnp.einsum("xzy,yb->xzb", spectrum, table_y, precision=highest)
        lined = lax.all_to_all(across, "chan", split_axis=2, concat_axis=0, tiled=True)
        lined = jnp.einsum("ax,xzy->azy", table_x, lined, precision=highest)
        eigen_part = lax.dynamic_slice_in_dim(eigen_y, chan_place * width_piece, width_piece)
        lined = lined / (
            conduct_ref
            * (eigen_x[:, None, None] + eigen_z[None, :, None] + eigen_part[None, None, :])
        )
        lined = jnp.einsum("ax,xzy->azy", table_x, lined, precision=highest)
        across = lax.all_to_all(lined, "chan", split_axis=0, concat_axis=2, tiled=True)
        spectrum = jnp.einsum("xzy,yb->xzb", across, table_y, precision=highest)
        spectrum = lax.all_to_all(spectrum, "wide", split_axis=2, concat_axis=1, tiled=True)
        potential_field = potential_field + jnp.einsum(
            "az,xzy->xay", table_z, spectrum, precision=highest
        )
    cell_rows = concs.reshape(species_all, -1).T
    junction_sums = jax.ops.segment_sum(cell_rows, owners, num_segments=junction_total + 1)
    junction_sums, total_counts = lax.psum((junction_sums, cell_counts), ("chan", "wide"))
    means = junction_sums / jnp.maximum(total_counts, 1.0)[:, None]
    own_means = means[:junction_total]
    table = coupling * (own_means[partner] - own_means)
    table = jnp.concatenate([table, jnp.zeros((1, species_all), jnp.float32)], axis=0)
    source = table[owners].T.reshape(concs.shape)
    conc_fixed = rim_replace(conc_raw, lower_x, upper_x, lower_y, upper_y)
    phi_fixed = rim_replace(halo_potential(potential_field), lower_x, upper_x, lower_y, upper_y)
    conc_near_all = neighbours(conc_fixed, "edge")
    phi_near_all = neighbours(phi_fixed, "edge")
    diagonal_part = jnp.zeros_like(concs) + 1.5 / time_step
    gathered_terms = (4.0 * conc_now - conc_prev) / (2.0 * time_step) + source
    for conc_near, phi_near in zip(conc_near_all, phi_near_all):
        velocity = drift * (potential_field - phi_near)[None]
        diagonal_part = diagonal_part + spread + jnp.maximum(velocity, 0.0)
        gathered_terms = gathered_terms + (spread + jnp.maximum(-velocity, 0.0)) * conc_near
    concs = gathered_terms / diagonal_part
    return (concs, potential_field)


def solution(mesh):
    return jax.shard_map(
        per_device,
        mesh=mesh,
        in_specs=(
            P(None, "chan", None, "wide"),
            P(None, "chan", None, "wide"),
            P("chan", None, "wide"),
            P("chan", None, "wide"),
            P(),
            P(),
            P(),
        ),
        out_specs=(P(None, "chan", None, "wide"), P("chan", None, "wide")),
        check_vma=False,
    )
```

profile of v0, /device:TPU:1, one launch (start us, length us, event | category | flops | bytes accessed | tf_op | source)
XLA Modules:
  0.0 883.1 jit_solution(6742743469902880809)
XLA Ops:
  9.0 4.6 collective-permute-start.24
  26.8 3.6 collective-permute-start
  37.8 4.8 collective-permute-start.5
  46.5 10.9 %all-to-all-start = ((f32[2,64,128]{2,0,1:T(2,128)}), f32[2,64,128]{2,0,1:T(2,128)S(1)}, u32[]{:S(2)}, u32[]{:S(2)}) async-start(f32[2,64,128]{2,0,1:T(2,128)} %copy.85), calls=%async_computation | async-start | bytes 131072 | tf_op jit(solution)/shard_map/all_to_all | solution.py:125
  57.4 7.1 all-to-all-done
  64.6 16.9 %fusion.14 = f32[2,8,1024]{2,1,0:T(8,128)S(1)} fusion(f32[1024]{0:T(1024)S(1)} %get-tuple-element.64, f32[1024]{0:T(1024)S(1)} %get-tuple-element.65, f32[2,8,8,128]{3,0,2,1:T(2,128)S(1)} %bitcast.241), kind=kOutput, calls=%fused_computation.18 | convolution fusion | flops 204472320 | bytes 139264 | tf_op jit(solution)/shard_map/xzy,yb->xzb/dot_general | solution.py:126
  84.2 11.9 %all-to-all-start.1 = ((f32[32,1,512]{2,1,0:T(1,128)}), f32[32,1,512]{2,1,0:T(1,128)S(1)}, u32[]{:S(2)}, u32[]{:S(2)}) async-start(f32[32,1,512]{2,1,0:T(1,128)} %reshape.171), calls=%async_computation.1 | async-start | bytes 131072 | tf_op jit(solution)/shard_map/all_to_all | solution.py:127
  96.3 7.2 all-to-all-done.1
  108.4 10.9 %all_to_all.288 = f32[32,1,512]{2,1,0:T(1,128)S(1)} all-to-all(f32[32,1,512]{2,1,0:T(1,128)S(1)} %reshape.173), channel_id=1, replica_groups=mesh['chan'=32,'wide'=8] {'chan'}, dimensions={0} | all-to-all | bytes 131072 | tf_op jit(solution)/shard_map/all_to_all | solution.py:135
  120.4 16.6 %fusion.12 = f32[2,8,1024]{2,1,0:T(8,128)S(1)} fusion(f32[2,8,1024]{2,1,0:T(8,128)S(1)} %all_to_all.219, f32[1024]{0:T(1024)S(1)} %get-tuple-element.64, f32[1024]{0:T(1024)S(1)} %get-tuple-element.65), kind=kOutput, calls=%fused_computation.16 | convolution fusion | flops 204472320 | bytes 139264 | tf_op jit(solution)/shard_map/xzy,yb->xzb/dot_general | solution.py:136
  139.1 9.5 %all_to_all.289 = f32[8,1,2048]{2,1,0:T(1,128)S(1)} all-to-all(f32[8,1,2048]{2,1,0:T(1,128)S(1)} %reshape.175), channel_id=1, replica_groups=mesh['chan'=32,'wide'=8] {'wide'}, dimensions={0} | all-to-all | bytes 131072 | tf_op jit(solution)/shard_map/all_to_all | solution.py:137
  159.9 4.0 collective-permute-start.10
  166.8 12.9 %all_to_all.290 = f32[2,64,128]{2,0,1:T(2,128)S(1)} all-to-all(f32[2,64,128]{2,0,1:T(2,128)S(1)} %copy.94), channel_id=1, replica_groups=mesh['chan'=32,'wide'=8] {'wide'}, dimensions={1} | all-to-all | bytes 131072 | tf_op jit(solution)/shard_map/all_to_all | solution.py:125
  179.7 16.6 %fusion.10 = f32[2,8,1024]{2,1,0:T(8,128)S(1)} fusion(f32[1024]{0:T(1024)S(1)} %get-tuple-element.64, f32[1024]{0:T(1024)S(1)} %get-tuple-element.65, f32[2,8,8,128]{3,0,2,1:T(2,128)S(1)} %bitcast.244), kind=kOutput, calls=%fused_computation.14 | convolution fusion | flops 204472320 | bytes 139264 | tf_op jit(solution)/shard_map/xzy,yb->xzb/dot_general | solution.py:126
  199.0 9.6 %all-to-all-start.5 = ((f32[32,1,512]{2,1,0:T(1,128)}), f32[32,1,512]{2,1,0:T(1,128)S(1)}, u32[]{:S(2)}, u32[]{:S(2)}) async-start(f32[32,1,512]{2,1,0:T(1,128)} %reshape.177), calls=%async_computation.5 | async-start | bytes 131072 | tf_op jit(solution)/shard_map/all_to_all | solution.py:127
  210.8 5.2 all-to-all-done.5
  220.9 3.9 all-to-all-start.6
  225.8 4.6 copy.125
  230.4 111.6 %scatter_custom_fusion = f32[2049,8]{1,0:T(8,128)} fusion(s32[16384]{0:T(1024)S(1)} %bitcast.237, f32[16384,8]{1,0:T(8,128)} %bitcast.196, f32[]{:T(128)} %constant.28.clone.1), kind=kCustom, calls=%fused_computation.84 | custom fusion | flops 131072 | bytes 66080 | tf_op jit(solution)/shard_map/scatter-add | solution.py:142
  343.2 16.8 %fusion.8 = f32[2,8,1024]{2,1,0:T(8,128)S(1)} fusion(f32[2,8,1024]{2,1,0:T(8,128)S(1)} %all_to_all.235, f32[1024]{0:T(1024)S(1)} %copy-done.21, f32[1024]{0:T(1024)S(1)} %copy-done.25), kind=kOutput, calls=%fused_computation.12 | convolution fusion | flops 204472320 | bytes 139264 | tf_op jit(solution)/shard_map/xzy,yb->xzb/dot_general | solution.py:136
  366.2 7.1 all-to-all-done.7
  378.5 3.6 collective-permute-start.12
  382.8 110.6 %scatter_custom_fusion.1 = f32[2049]{0:T(1024)S(1)} fusion(s32[16384]{0:T(1024)S(1)} %bitcast.239, f32[16384]{0:T(1024)S(1)} %broadcast.172, f32[]{:T(128)} %constant.28.clone.1), kind=kCustom, calls=%fused_computation.420 | custom fusion | flops 16384 | bytes 8200 | tf_op jit(solution)/shard_map/scatter-add | solution.py:107
  494.8 4.0 collective-permute-start.14
  498.8 75.3 %psum.15 = f32[2049]{0:T(1024)S(1)} all-reduce(f32[2049]{0:T(1024)S(1)} %scatter_custom_fusion.1), channel_id=1, replica_groups=mesh['chan'=32,'wide'=8] {'chan','wide'}, use_global_device_ids=true, to_apply=%region_3.0 | all-reduce | flops 2049 | bytes 16392 | tf_op jit(solution)/shard_map/psum | solution.py:143
  579.5 6.5 all-to-all-done.8
  585.9 17.3 %fusion.6 = f32[2,8,1024]{2,1,0:T(8,128)S(1)} fusion(f32[1024]{0:T(1024)} %copy-done.20, f32[1024]{0:T(1024)} %copy-done.24, f32[2,8,8,128]{3,0,2,1:T(2,128)S(1)} %bitcast.243), kind=kOutput, calls=%fused_computation.10 | convolution fusion | flops 204472320 | bytes 139264 | tf_op jit(solution)/shard_map/xzy,yb->xzb/dot_general | solution.py:126
  606.0 6.1 all-to-all-start.9
  612.1 7.4 all-to-all-done.9
  624.4 4.3 all-to-all-start.10
  628.8 7.0 all-to-all-done.10
  637.0 16.6 %fusion.4 = f32[2,8,1024]{2,1,0:T(8,128)S(1)} fusion(f32[2,8,1024]{2,1,0:T(8,128)S(1)} %all_to_all.251, f32[1024]{0:T(1024)S(1)} %copy-done.22, f32[1024]{0:T(1024)S(1)} %copy-done.26), kind=kOutput, calls=%fused_computation.8 | convolution fusion | flops 204472320 | bytes 139264 | tf_op jit(solution)/shard_map/xzy,yb->xzb/dot_general | solution.py:136
  661.3 7.6 gather_fusion
  680.8 4.6 collective-permute-start.18
  688.6 4.0 collective-permute-start.26
  694.7 6.2 all-to-all-start.12
  702.9 54.5 %gather_fusion.1 = f32[16384,8]{1,0:T(8,128)} fusion(f32[2049,8]{1,0:T(8,128)S(1)} %concatenate.143, s32[16384]{0:T(1024)S(1)} %copy-done.13), kind=kCustom, calls=%fused_computation.1 | custom fusion | bytes 1114112 | tf_op jit(solution)/shard_map/gather | solution.py:148
  757.4 6.1 copy.126
  766.3 16.8 %fusion.2 = f32[2,8,1024]{2,1,0:T(8,128)S(1)} fusion(f32[1024]{0:T(1024)S(1)} %copy-done.23, f32[1024]{0:T(1024)S(1)} %copy-done.27, f32[2,8,8,128]{3,0,2,1:T(2,128)S(1)} %bitcast.242), kind=kOutput, calls=%fused_computation.6 | convolution fusion | flops 204472320 | bytes 139264 | tf_op jit(solution)/shard_map/xzy,yb->xzb/dot_general | solution.py:126
  785.9 8.9 %all-to-all-start.13 = ((f32[32,1,512]{2,1,0:T(1,128)}), f32[32,1,512]{2,1,0:T(1,128)S(1)}, u32[]{:S(2)}, u32[]{:S(2)}) async-start(f32[32,1,512]{2,1,0:T(1,128)} %reshape.189), calls=%async_computation.13 | async-start | bytes 131072 | tf_op jit(solution)/shard_map/all_to_all | solution.py:127
  797.2 4.9 all-to-all-done.13
  807.1 4.1 all-to-all-start.14
  812.4 6.1 all-to-all-done.14
  819.6 16.6 %fusion = f32[2,8,1024]{2,1,0:T(8,128)S(1)} fusion(f32[2,8,1024]{2,1,0:T(8,128)S(1)} %all_to_all.267, f32[1024]{0:T(1024)S(1)} %copy-done.23, f32[1024]{0:T(1024)S(1)} %copy-done.27), kind=kOutput, calls=%fused_computation.4 | convolution fusion | flops 204472320 | bytes 139264 | tf_op jit(solution)/shard_map/xzy,yb->xzb/dot_general | solution.py:136
  839.0 6.9 all-to-all-start.15
  847.3 5.9 all-to-all-done.15
  858.4 3.7 collective-permute-start.21
  866.8 4.0 collective-permute-start.22
  (277 shorter events, 151.3 us)
Async XLA Ops:
  9.0 14.6 %collective-permute-start.24 = (f32[8,1,64,128]{3,2,1,0:T(8,128)S(1)}, f32[8,1,64,128]{3,2,1,0:T(8,128)S(1)}, u32[]{:S(2)}, u32[]{:S(2)}) collective-permute-start(f32[8,1,64,128]{3,2,1,0:T(8,128)S(1)} %get-tuple-element.16), channel_id=1, source_target_pairs={{0,8},{8,16},{16,24},{24,32},{32,40},{40,48},{48,56},{56,64},{64,7... | collective-permute-start | bytes 786440 | tf_op jit(solution)/shard_map/ppermute | solution.py:26
  14.4 8.4 collective-permute-start.1
  16.3 14.2 %collective-permute-start.3 = (f32[1,64,128]{2,1,0:T(8,128)S(1)}, f32[1,64,128]{2,1,0:T(8,128)S(1)}, u32[]{:S(2)}, u32[]{:S(2)}) collective-permute-start(f32[1,64,128]{2,1,0:T(8,128)S(1)} %get-tuple-element.55), channel_id=1, source_target_pairs={{8,0},{16,8},{24,16},{32,24},{40,32},{48,40},{56,48},{64,56},{72,6... | collective-permute-start | bytes 98312 | tf_op jit(solution)/shard_map/ppermute | solution.py:28
  24.8 549.3 %copy-start.6 = (f32[2,64,128]{2,1,0:T(8,128)}, f32[2,64,128]{2,1,0:T(8,128)S(1)}, u32[]{:S(2)}) copy-start(f32[2,64,128]{2,1,0:T(8,128)S(1)} %get-tuple-element.4) | copy-start | bytes 196612
  24.8 5.6 collective-permute-start.2
  26.8 4.7 collective-permute-start
  30.5 135.8 %copy-start.7 = (f32[1,64,128]{2,1,0:T(8,128)}, f32[1,64,128]{2,1,0:T(8,128)S(1)}, u32[]{:S(2)}) copy-start(f32[1,64,128]{2,1,0:T(8,128)S(1)} %collective-permute-done.2) | copy-start | bytes 98308
  31.4 134.9 %copy-start.9 = (f32[1,64,128]{2,1,0:T(8,128)}, f32[1,64,128]{2,1,0:T(8,128)S(1)}, u32[]{:S(2)}) copy-start(f32[1,64,128]{2,1,0:T(8,128)S(1)} %collective-permute-done) | copy-start | bytes 98308
  31.5 11.1 %collective-permute-start.4 = (f32[4,64,1]{2,1,0:T(8,128)S(1)}, f32[4,64,1]{2,1,0:T(8,128)S(1)}, u32[]{:S(2)}, u32[]{:S(2)}) collective-permute-start(f32[4,64,1]{2,1,0:T(8,128)S(1)} %get-tuple-element.37), channel_id=1, source_target_pairs={{0,1},{1,2},{2,3},{3,4},{4,5},{5,6},{6,7},{8,9},{9,10},{10,11},{11... | collective-permute-start | bytes 3080 | tf_op jit(solution)/shard_map/ppermute | solution.py:26
  35.1 7.5 collective-permute-start.6
  36.5 7.9 collective-permute-start.7
  37.8 7.6 collective-permute-start.5
  46.5 18.1 %all-to-all-start = ((f32[2,64,128]{2,0,1:T(2,128)}), f32[2,64,128]{2,0,1:T(2,128)S(1)}, u32[]{:S(2)}, u32[]{:S(2)}) async-start(f32[2,64,128]{2,0,1:T(2,128)} %copy.85), calls=%async_computation | async-start | bytes 131072 | tf_op jit(solution)/shard_map/all_to_all | solution.py:125
  57.4 122.3 %copy-start.24 = (f32[1024]{0:T(1024)}, f32[1024]{0:T(1024)S(1)}, u32[]{:S(2)}) copy-start(f32[1024]{0:T(1024)S(1)} %get-tuple-element.65) | copy-start | bytes 12292
  84.2 19.3 %all-to-all-start.1 = ((f32[32,1,512]{2,1,0:T(1,128)}), f32[32,1,512]{2,1,0:T(1,128)S(1)}, u32[]{:S(2)}, u32[]{:S(2)}) async-start(f32[32,1,512]{2,1,0:T(1,128)} %reshape.171), calls=%async_computation.1 | async-start | bytes 131072 | tf_op jit(solution)/shard_map/all_to_all | solution.py:127
  151.9 5.6 collective-permute-start.9
  155.4 3.1 collective-permute-start.8
  158.6 6.8 collective-permute-start.11
  159.9 6.4 collective-permute-start.10
  199.0 16.9 %all-to-all-start.5 = ((f32[32,1,512]{2,1,0:T(1,128)}), f32[32,1,512]{2,1,0:T(1,128)S(1)}, u32[]{:S(2)}, u32[]{:S(2)}) async-start(f32[32,1,512]{2,1,0:T(1,128)} %reshape.177), calls=%async_computation.5 | async-start | bytes 131072 | tf_op jit(solution)/shard_map/all_to_all | solution.py:127
  208.6 469.1 %collective-permute-start.25 = (f32[8,1,64,128]{3,2,1,0:T(8,128)}, f32[8,1,64,128]{3,2,1,0:T(8,128)}, u32[]{:S(2)}, u32[]{:S(2)}) collective-permute-start(f32[8,1,64,128]{3,2,1,0:T(8,128)} %get-tuple-element.15), channel_id=1, source_target_pairs={{8,0},{16,8},{24,16},{32,24},{40,32},{48,40},{56,48},{64,56},{72,6... | collective-permute-start | bytes 786440 | tf_op jit(solution)/shard_map/ppermute | solution.py:28
  220.9 121.1 %all-to-all-start.6 = ((f32[32,1,512]{2,1,0:T(1,128)}), f32[32,1,512]{2,1,0:T(1,128)S(1)}, u32[]{:S(2)}, u32[]{:S(2)}) async-start(f32[32,1,512]{2,1,0:T(1,128)} %reshape.179), calls=%async_computation.6 | async-start | bytes 131072 | tf_op jit(solution)/shard_map/all_to_all | solution.py:135
  224.9 434.8 %all-reduce.8.cloned.1.call-start = ((), (), s32[]{:S(2)}) async-start(), calls=%async_computation.16 | async-start | bytes 2105344 | tf_op jit(solution)/shard_map/psum | solution.py:143
  360.0 214.1 %copy-start.8 = (f32[1,64,128]{2,1,0:T(8,128)S(1)}, f32[1,64,128]{2,1,0:T(8,128)}, u32[]{:S(2)}) copy-start(f32[1,64,128]{2,1,0:T(8,128)} %copy-done.7) | copy-start | bytes 98308
  360.0 214.1 %copy-start.10 = (f32[1,64,128]{2,1,0:T(8,128)S(1)}, f32[1,64,128]{2,1,0:T(8,128)}, u32[]{:S(2)}) copy-start(f32[1,64,128]{2,1,0:T(8,128)} %copy-done.9) | copy-start | bytes 98308
  362.8 10.6 %all-to-all-start.7 = ((f32[8,1,2048]{2,1,0:T(1,128)}), f32[8,1,2048]{2,1,0:T(1,128)S(1)}, u32[]{:S(2)}, u32[]{:S(2)}) async-start(f32[8,1,2048]{2,1,0:T(1,128)} %reshape.181), calls=%async_computation.7 | async-start | bytes 131072 | tf_op jit(solution)/shard_map/all_to_all | solution.py:137
  376.5 116.8 %collective-permute-start.13 = (f32[1,64,128]{2,1,0:T(8,128)S(1)}, f32[1,64,128]{2,1,0:T(8,128)S(1)}, u32[]{:S(2)}, u32[]{:S(2)}) collective-permute-start(f32[1,64,128]{2,1,0:T(8,128)S(1)} %get-tuple-element.50), channel_id=1, source_target_pairs={{8,0},{16,8},{24,16},{32,24},{40,32},{48,40},{56,48},{64,56},{72,6... | collective-permute-start | bytes 98312 | tf_op jit(solution)/shard_map/ppermute | solution.py:28
  378.5 114.9 %collective-permute-start.12 = (f32[1,64,128]{2,1,0:T(8,128)S(1)}, f32[1,64,128]{2,1,0:T(8,128)S(1)}, u32[]{:S(2)}, u32[]{:S(2)}) collective-permute-start(f32[1,64,128]{2,1,0:T(8,128)S(1)} %get-tuple-element.49), channel_id=1, source_target_pairs={{0,8},{8,16},{16,24},{24,32},{32,40},{40,48},{48,56},{56,64},{64,7... | collective-permute-start | bytes 98312 | tf_op jit(solution)/shard_map/ppermute | solution.py:26
  493.5 80.6 %collective-permute-start.15 = (f32[4,64,1]{2,1,0:T(8,128)S(1)}, f32[4,64,1]{2,1,0:T(8,128)S(1)}, u32[]{:S(2)}, u32[]{:S(2)}) collective-permute-start(f32[4,64,1]{2,1,0:T(8,128)S(1)} %get-tuple-element.30), channel_id=1, source_target_pairs={{1,0},{2,1},{3,2},{4,3},{5,4},{6,5},{7,6},{9,8},{10,9},{11,10},{12... | collective-permute-start | bytes 3080 | tf_op jit(solution)/shard_map/ppermute | solution.py:28
  494.8 79.3 %collective-permute-start.14 = (f32[4,64,1]{2,1,0:T(8,128)S(1)}, f32[4,64,1]{2,1,0:T(8,128)S(1)}, u32[]{:S(2)}, u32[]{:S(2)}) collective-permute-start(f32[4,64,1]{2,1,0:T(8,128)S(1)} %get-tuple-element.29), channel_id=1, source_target_pairs={{0,1},{1,2},{2,3},{3,4},{4,5},{5,6},{6,7},{8,9},{9,10},{10,11},{11... | collective-permute-start | bytes 3080 | tf_op jit(solution)/shard_map/ppermute | solution.py:26
  575.3 10.7 %all-to-all-start.8 = ((f32[2,64,128]{2,0,1:T(2,128)}), f32[2,64,128]{2,0,1:T(2,128)S(1)}, u32[]{:S(2)}, u32[]{:S(2)}) async-start(f32[2,64,128]{2,0,1:T(2,128)} %copy.103), calls=%async_computation.8 | async-start | bytes 131072 | tf_op jit(solution)/shard_map/all_to_all | solution.py:125
  606.0 13.4 %all-to-all-start.9 = ((f32[32,1,512]{2,1,0:T(1,128)}), f32[32,1,512]{2,1,0:T(1,128)S(1)}, u32[]{:S(2)}, u32[]{:S(2)}) async-start(f32[32,1,512]{2,1,0:T(1,128)} %reshape.183), calls=%async_computation.9 | async-start | bytes 131072 | tf_op jit(solution)/shard_map/all_to_all | solution.py:127
  624.4 11.4 %all-to-all-start.10 = ((f32[32,1,512]{2,1,0:T(1,128)}), f32[32,1,512]{2,1,0:T(1,128)S(1)}, u32[]{:S(2)}, u32[]{:S(2)}) async-start(f32[32,1,512]{2,1,0:T(1,128)} %reshape.185), calls=%async_computation.10 | async-start | bytes 131072 | tf_op jit(solution)/shard_map/all_to_all | solution.py:135
  656.3 12.6 %all-to-all-start.11 = ((f32[8,1,2048]{2,1,0:T(1,128)}), f32[8,1,2048]{2,1,0:T(1,128)S(1)}, u32[]{:S(2)}, u32[]{:S(2)}) async-start(f32[8,1,2048]{2,1,0:T(1,128)} %reshape.187), calls=%async_computation.11 | async-start | bytes 131072 | tf_op jit(solution)/shard_map/all_to_all | solution.py:137
  672.1 6.6 collective-permute-start.17
  674.4 4.3 collective-permute-start.16
  679.5 13.1 %collective-permute-start.19 = (f32[4,64,1]{2,1,0:T(8,128)}, f32[4,64,1]{2,1,0:T(8,128)}, u32[]{:S(2)}, u32[]{:S(2)}) collective-permute-start(f32[4,64,1]{2,1,0:T(8,128)} %get-tuple-element.28), channel_id=1, source_target_pairs={{1,0},{2,1},{3,2},{4,3},{5,4},{6,5},{7,6},{9,8},{10,9},{11,10},{12... | collective-permute-start | bytes 3080 | tf_op jit(solution)/shard_map/ppermute | solution.py:28
  680.8 11.8 %collective-permute-start.18 = (f32[4,64,1]{2,1,0:T(8,128)}, f32[4,64,1]{2,1,0:T(8,128)}, u32[]{:S(2)}, u32[]{:S(2)}) collective-permute-start(f32[4,64,1]{2,1,0:T(8,128)} %get-tuple-element.27), channel_id=1, source_target_pairs={{0,1},{1,2},{2,3},{3,4},{4,5},{5,6},{6,7},{8,9},{9,10},{10,11},{11... | collective-permute-start | bytes 3080 | tf_op jit(solution)/shard_map/ppermute | solution.py:26
  686.8 76.7 %collective-permute-start.27 = (f32[8,4,64,1]{2,0,3,1:T(8,128)}, f32[8,4,64,1]{2,0,3,1:T(8,128)S(1)}, u32[]{:S(2)}, u32[]{:S(2)}) collective-permute-start(f32[8,4,64,1]{2,0,3,1:T(8,128)} %copy.122), channel_id=1, source_target_pairs={{1,0},{2,1},{3,2},{4,3},{5,4},{6,5},{7,6},{9,8},{10,9},{11,10},{12... | collective-permute-start | bytes 24584 | tf_op jit(solution)/shard_map/ppermute | solution.py:28
  688.6 76.3 %collective-permute-start.26 = (f32[8,4,64,1]{2,0,3,1:T(8,128)S(1)}, f32[8,4,64,1]{2,0,3,1:T(8,128)S(1)}, u32[]{:S(2)}, u32[]{:S(2)}) collective-permute-start(f32[8,4,64,1]{2,0,3,1:T(8,128)S(1)} %copy.121), channel_id=1, source_target_pairs={{0,1},{1,2},{2,3},{3,4},{4,5},{5,6},{6,7},{8,9},{9,10},{10,11},{11... | collective-permute-start | bytes 24584 | tf_op jit(solution)/shard_map/ppermute | solution.py:26
  694.7 71.6 %all-to-all-start.12 = ((f32[2,64,128]{2,0,1:T(2,128)}), f32[2,64,128]{2,0,1:T(2,128)S(1)}, u32[]{:S(2)}, u32[]{:S(2)}) async-start(f32[2,64,128]{2,0,1:T(2,128)} %copy.112), calls=%async_computation.12 | async-start | bytes 131072 | tf_op jit(solution)/shard_map/all_to_all | solution.py:125
  785.9 16.3 %all-to-all-start.13 = ((f32[32,1,512]{2,1,0:T(1,128)}), f32[32,1,512]{2,1,0:T(1,128)S(1)}, u32[]{:S(2)}, u32[]{:S(2)}) async-start(f32[32,1,512]{2,1,0:T(1,128)} %reshape.189), calls=%async_computation.13 | async-start | bytes 131072 | tf_op jit(solution)/shard_map/all_to_all | solution.py:127
  807.1 11.4 %all-to-all-start.14 = ((f32[32,1,512]{2,1,0:T(1,128)}), f32[32,1,512]{2,1,0:T(1,128)S(1)}, u32[]{:S(2)}, u32[]{:S(2)}) async-start(f32[32,1,512]{2,1,0:T(1,128)} %reshape.191), calls=%async_computation.14 | async-start | bytes 131072 | tf_op jit(solution)/shard_map/all_to_all | solution.py:135
  839.0 14.2 %all-to-all-start.15 = ((f32[8,1,2048]{2,1,0:T(1,128)}), f32[8,1,2048]{2,1,0:T(1,128)S(1)}, u32[]{:S(2)}, u32[]{:S(2)}) async-start(f32[8,1,2048]{2,1,0:T(1,128)} %reshape.193), calls=%async_computation.15 | async-start | bytes 131072 | tf_op jit(solution)/shard_map/all_to_all | solution.py:137
  858.4 6.9 collective-permute-start.21
  862.1 3.2 collective-permute-start.20
  865.4 6.7 collective-permute-start.23
  866.8 6.2 collective-permute-start.22
  (25 other events, 690.8 us)
Sparse Core Ops, SparseCore 0:
  342.1 253.6 all-reduce.7
where the time goes:
time: 899 us; the launch traced here: 883 us
  other arithmetic  251 us (28%)
  starting transfers between devices  160 us (18%)
  matrix products  142 us (16%)
  local copies, waits for them, and re-layouts  132 us (15%)
  blocking collectives  109 us (12%)
  waiting for transfers between devices  73.7 us (8%)
  between operations  16 us (2%)
    scatter-add x1, other arithmetic, per_device(): jax.ops.segment_sum(cell_rows, owners, num_segments=junction_total + 1)  112 us
    scatter-add x1, other arithmetic, per_device(): jax.ops.segment_sum(jnp.ones(owners.shape, jnp.float32), owners, num_segm...  111 us
    psum x1, blocking collectives, per_device(): lax.psum((junction_sums, cell_counts), ('chan', 'wide'))  75.3 us
    dot_general x4, matrix products, per_device(): across = jnp.einsum('xzy,yb->xzb', spectrum, table_y, precision=highest)  67.5 us
    dot_general x4, matrix products, per_device(): spectrum = jnp.einsum('xzy,yb->xzb', across, table_y, precision=highest)  66.6 us
    gather x1, local copies, waits for them, and re-layouts, per_device(): source = table[owners].T.reshape(concs.shape)  54.5 us
    ppermute x14, starting transfers between devices, with_halo(): lax.ppermute(tail, axis, [(i, (i + 1) % count) for i in range(ends)])  50.2 us
    all_to_all x4, starting transfers between devices, per_device(): lax.all_to_all(across, 'chan', split_axis=2, concat_axis=0, tiled=True)  36.4 us
  transfers between devices with their start and end apart: 42, of which 18 were waited for; matrix products, arithmetic and copies ran while one was open for 45% of the time, Pallas kernels for 0%

commit v1 on v0

v1 whole, which is shorter than its diff:
```python
import functools

import jax
import jax.numpy as jnp
import numpy as np
from jax import lax
from jax.experimental import pallas as pl
from jax.experimental.pallas import tpu as pltpu
from jax.sharding import PartitionSpec as P

SWEEPS = 4
charge_scale = 0.05
coupling = 2.0
conduct_ref = 1.5
LANES = 128
LEVELS = 16
ROWS_AT_ONCE = 4
MESH = pl.DeviceIdType.MESH
f32 = jnp.float32
bf16 = jnp.bfloat16


def sine_table(length):
    index = np.arange(length) + 1.0
    return np.sqrt(2.0 / (length + 1.0)) * np.sin(np.pi * np.outer(index, index) / (length + 1.0))


def eigen_values(length):
    return 2.0 - 2.0 * np.cos(np.pi * (np.arange(length) + 1.0) / (length + 1.0))


def halves(table):
    table = np.asarray(table, np.float32)
    high = table.astype(bf16)
    low = (table - high.astype(np.float32)).astype(bf16)
    return high, low


def make_tables(nc, cx, nz, cy):
    nx, nb = nc * cx, nz // nc
    qx, qz, qy = sine_table(nx), sine_table(nz), sine_table(cy)
    depth_to = np.zeros((nc, cx, nb, cx, nz))
    for x in range(cx):
        depth_to[:, x, :, x, :] = qz.reshape(nc, nb, nz)
    length_to = np.einsum("aX,bc->abXc", qx, np.eye(nb)) / conduct_ref
    length_back = np.zeros((nc, cx + 2, nb, nx, nb))
    for p in range(nc):
        for xx in range(cx + 2):
            place = cx * p + xx - 1
            if 0 <= place < nx:
                for b in range(nb):
                    length_back[p, xx, b, :, b] = qx[place]
    depth_back = np.zeros((cx + 2, nz, nc, cx + 2, nb))
    for xx in range(cx + 2):
        depth_back[xx, :, :, xx, :] = qz.reshape(nz, nc, nb)
    modes = nx * nb
    lam = eigen_values(nx)[:, None] + eigen_values(nz)[None, :]
    lam = lam.reshape(nx, nc, nb).transpose(1, 0, 2).reshape(nc, 1, modes)
    theta = np.arccosh(1.0 + lam / 2.0)
    return dict(
        depth_to=halves(depth_to.reshape(nc * cx * nb, cx * nz)),
        length_to=halves(length_to.reshape(modes, modes)),
        length_back=halves(length_back.reshape(nc * (cx + 2) * nb, modes)),
        length_back_f=np.asarray(length_back.reshape(nc * (cx + 2) * nb, modes), np.float32),
        depth_back=halves(depth_back.reshape((cx + 2) * nz, nc * (cx + 2) * nb)),
        width=halves(qy),
        lam=np.asarray(lam, np.float32),
        theta=np.asarray(theta, np.float32),
        lam_y=np.asarray(eigen_values(cy)[None, :], np.float32),
    )


def dot(a, b):
    return jnp.dot(a, b, preferred_element_type=f32)


def split(value):
    high = value.astype(bf16)
    return high, (value - high.astype(f32)).astype(bf16)


def product(table, value):
    high, low = split(value)
    return dot(table[0], high) + dot(table[1], high) + dot(table[0], low)


def product_right(value, table):
    high, low = split(value)
    return dot(high, table[0]) + dot(high, table[1]) + dot(low, table[0])


def iota(shape, dim):
    return lax.broadcasted_iota(jnp.int32, shape, dim)


def kernel(
    cfg,
    val_ref, dif_ref, conc_ref, prev_ref, phi_ref, own_ref, par_ref,
    lam_ref, theta_ref, lam_y_ref,
    dt_h, dt_l, lt_h, lt_l, lb_h, lb_l, lb_f, db_h, db_l, wy_h, wy_l,
    out_conc, out_phi,
    phi_e, faces, charge, tab_p, tab_m, tab_d, edge_h, edge_l, coef,
    send1, recv1, send_g, recv_g, send2, recv2,
    sig, cols, cols_in, plane_in, conc_in,
    jacc, jmean, jrecv, jsum, jwide, jpiece, jall, jtab, src,
    send_sem, recv_sem,
):
    nc, nw, cx, nz, cy = cfg
    nb = nz // nc
    rows = cx * nz
    modes = nc * cx * nb
    species = conc_ref.shape[0] // rows
    me_c = lax.axis_index("chan")
    me_w = lax.axis_index("wide")
    left_c, right_c = lax.rem(me_c + nc - 1, nc), lax.rem(me_c + 1, nc)
    left_w, right_w = lax.rem(me_w + nw - 1, nw), lax.rem(me_w + 1, nw)

    barrier = pltpu.get_barrier_semaphore()

    def greet_c(i, _):
        pl.semaphore_signal(barrier, inc=1, device_id={"chan": lax.rem(me_c + i, nc)}, device_id_type=MESH)
        return 0

    def greet_w(i, _):
        pl.semaphore_signal(barrier, inc=1, device_id={"wide": lax.rem(me_w + i, nw)}, device_id_type=MESH)
        return 0

    lax.fori_loop(1, nc, greet_c, 0)
    lax.fori_loop(1, nw, greet_w, 0)

    lane = iota((rows, cy), 1)
    row = iota((rows, cy), 0)
    depth = lax.rem(row, nz)
    at_first, at_last = lane == 0, lane == cy - 1
    top, bottom = depth == 0, depth == nz - 1

    val = [val_ref[s].astype(f32) for s in range(species)]
    dif = [dif_ref[s] for s in range(species)]
    total = jnp.zeros((rows, cy), f32)
    part = jnp.zeros((rows, cy), f32)
    weight_all = jnp.float32(0.0)
    for s in range(species):
        c = conc_ref[pl.ds(s * rows, rows), :]
        square = val[s] * val[s]
        weight_all = weight_all + (square + 1.0) * dif[s]
        part = part + (square * dif[s]) * c * c
        total = total + val[s] * c
    sigma = 1.0 + part / jnp.full((1, 1), weight_all, f32)
    sig[...] = sigma
    charge[...] = charge_scale * total
    phi = phi_ref[...]

    packed = jnp.zeros((rows, cy), f32)
    for k in range(species + 2):
        field = phi if k == 0 else sigma if k == 1 else conc_ref[pl.ds((k - 2) * rows, rows), :]
        packed = jnp.where(lane == k, pltpu.roll(field, k, 1) if k else field, packed)
        packed = jnp.where(lane == LEVELS + k, pltpu.roll(field, LEVELS + 1 + k, 1), packed)
    cols[...] = packed.T[: 2 * LEVELS]

    pl.semaphore_wait(barrier, nc - 1 + nw - 1)

    SEM_A, SEM_G, SEM_B = 0, SWEEPS, 2 * SWEEPS
    SEM_H = 3 * SWEEPS
    SEM_J = SEM_H + 8

    def remote(src, dst, k, axis, place):
        return pltpu.make_async_remote_copy(
            src_ref=src, dst_ref=dst, send_sem=send_sem.at[k], recv_sem=recv_sem.at[k],
            device_id={axis: place}, device_id_type=MESH,
        )

    halo = [
        remote(cols.at[pl.ds(0, LEVELS)], cols_in.at[1], SEM_H, "wide", left_w),
        remote(cols.at[pl.ds(LEVELS, LEVELS)], cols_in.at[0], SEM_H + 1, "wide", right_w),
        remote(sig.at[pl.ds(0, nz)], plane_in.at[1, 0], SEM_H + 2, "chan", left_c),
        remote(sig.at[pl.ds(rows - nz, nz)], plane_in.at[0, 0], SEM_H + 3, "chan", right_c),
        remote(phi_ref.at[pl.ds(0, nz)], plane_in.at[1, 1], SEM_H + 4, "chan", left_c),
        remote(phi_ref.at[pl.ds(rows - nz, nz)], plane_in.at[0, 1], SEM_H + 5, "chan", right_c),
    ]
    conc_halo = []
    for s in range(species):
        conc_halo += [
            remote(conc_ref.at[pl.ds(s * rows, nz)], conc_in.at[1, s], SEM_H + 6, "chan", left_c),
            remote(conc_ref.at[pl.ds((s + 1) * rows - nz, nz)], conc_in.at[0, s], SEM_H + 7, "chan", right_c),
        ]
    for copy in halo:
        copy.start()

    def spread(src, dst, k, axis):
        n, me = (nc, me_c) if axis == "chan" else (nw, me_w)

        def body(i, _):
            p = lax.rem(me + i, n)
            remote(src(p), dst.at[me], k, axis, p).start()
            return 0

        lax.fori_loop(1, n, body, 0)
        pltpu.make_async_copy(src(me), dst.at[me], recv_sem.at[k]).start()

    def arrived(dst, k):
        pltpu.make_async_copy(dst, dst, recv_sem.at[k]).wait()

    def left(ref, k, n):
        part_of = ref.at[pl.ds(0, n)]
        pltpu.make_async_copy(part_of, part_of, send_sem.at[k]).wait()

    theta_row = theta_ref[me_c]
    theta = jnp.broadcast_to(theta_row, (cy, modes)).T
    lam = jnp.broadcast_to(lam_ref[me_c], (cy, modes)).T
    tab_d[...] = 1.0 / (lam + lam_y_ref[...])
    place = iota((modes, cy), 1).astype(f32)
    power = lambda n: jnp.exp(-theta * n)
    tab_p[...] = power(place)
    tab_m[...] = power(cy - 1.0 - place)
    scale = 1.0 / (1.0 - power(2.0 * cy + 2.0))
    mlane = iota((modes, cy), 1)
    edge_left = (power(place + 1.0) - power(2.0 * cy + 1.0 - place)) * scale
    edge_right = (power(cy - place) - power(cy + 2.0 + place)) * scale
    for k, edge in enumerate((edge_left, edge_right)):
        high, low = split(edge)
        here = pl.ds(k * modes, modes)
        edge_h[here, pl.ds(0, cy)] = high
        edge_l[here, pl.ds(0, cy)] = low
        edge_h[here, pl.ds(cy, cy)] = jnp.where(mlane == (cy - 1 if k == 0 else 0), 1.0, 0.0).astype(bf16)
        edge_l[here, pl.ds(cy, cy)] = jnp.zeros((modes, cy), bf16)
    width1 = cy * nw + 1
    rowp = lambda n: jnp.exp(-theta_row * n)
    front = 1.0 / ((1.0 - rowp(2.0)) * (1.0 - rowp(2.0 * width1)))
    for k in range(2):
        at = (cy * me_w if k == 0 else cy * (me_w + 1) + 1).astype(f32)
        below = (1.0 - rowp(2.0 * (width1 - at))) * front
        above = (1.0 - rowp(2.0 * at)) * front
        for w in range(nw):
            lower = (w < me_w) if k == 0 else (w <= me_w)
            n_plus = jnp.where(lower, at + (cy * w + 2.0), cy * w + 2.0 - at)
            n_minus = jnp.where(lower, at - (cy * w + cy - 1.0), 2.0 * width1 - at - (cy * w + cy - 1.0))
            factor = jnp.where(lower, below, above)
            sign = jnp.where(lower, -1.0, 1.0)
            coef[k, w, 0:1, :] = sign * factor * rowp(n_plus)
            coef[k, w, 1:2, :] = -sign * factor * rowp(n_minus)

    for copy in halo:
        copy.wait_recv()
    wall_xl, wall_xr = me_c == 0, me_c == nc - 1
    wall_yl, wall_yr = me_w == 0, me_w == nw - 1
    keep_xl, keep_xr = jnp.where(wall_xl, 0.0, 1.0), jnp.where(wall_xr, 0.0, 1.0)
    keep_yl, keep_yr = jnp.where(wall_yl, 0.0, 1.0), jnp.where(wall_yr, 0.0, 1.0)
    stacked = jnp.concatenate(
        [cols_in[0], cols_in[1], jnp.zeros((cy - 2 * LEVELS, rows), f32)], axis=0
    )
    col_in = stacked.T

    def neighbours(field, plane_l, plane_r, col_l, col_r, edge):
        low = field if edge is None else jnp.zeros_like(field)
        return [
            jnp.concatenate([plane_l, field[: rows - nz]], axis=0),
            jnp.concatenate([field[nz:], plane_r], axis=0),
            jnp.where(top, low, pltpu.roll(field, 1, 0)),
            jnp.where(bottom, low, pltpu.roll(field, rows - 1, 0)),
            jnp.where(at_first, col_l, pltpu.roll(field, 1, 1)),
            jnp.where(at_last, col_r, pltpu.roll(field, cy - 1, 1)),
        ]

    near = neighbours(
        sigma, plane_in[0, 0] * keep_xl, plane_in[1, 0] * keep_xr,
        col_in[:, 1:2] * keep_yl, col_in[:, LEVELS + 1 : LEVELS + 2] * keep_yr, 0,
    )
    for k in range(6):
        faces[k] = 0.5 * (sigma + near[k])
    phi_e[0:nz, 0:cy] = plane_in[0, 1] * keep_xl
    phi_e[nz : nz + rows, 0:cy] = phi
    phi_e[nz + rows : 2 * nz + rows, 0:cy] = plane_in[1, 1] * keep_xr
    phi_e[0:nz, cy : 2 * cy] = jnp.zeros((nz, cy), f32)
    phi_e[nz + rows : 2 * nz + rows, cy : 2 * cy] = jnp.zeros((nz, cy), f32)
    zero = jnp.zeros((rows, cy), f32)
    phi_e[nz : nz + rows, cy : 2 * cy] = jnp.where(
        at_last, col_in[:, 0:1] * keep_yl, jnp.where(at_first, col_in[:, LEVELS : LEVELS + 1] * keep_yr, zero)
    )

    def phi_near(beyond):
        field = phi_e[nz : nz + rows, 0:cy]
        ring = phi_e[nz : nz + rows, cy : 2 * cy]
        low = field if beyond is None else jnp.zeros_like(field)
        return field, [
            phi_e[0:rows, 0:cy],
            phi_e[2 * nz : 2 * nz + rows, 0:cy],
            jnp.where(top, low, pltpu.roll(field, 1, 0)),
            jnp.where(bottom, low, pltpu.roll(field, rows - 1, 0)),
            pltpu.roll(jnp.where(at_last, ring, field), 1, 1),
            pltpu.roll(jnp.where(at_first, ring, field), cy - 1, 1),
        ]

    def one_hot(label):
        return jnp.where(iota((LANES, LANES), 0) == (label & (LANES - 1)), 1.0, 0.0).astype(bf16)

    def sum_rows(first, last):
        def body(i, acc):
            picks, values = [], []
            for t in range(ROWS_AT_ONCE):
                r = i * ROWS_AT_ONCE + t
                label = own_ref[pl.ds(r, 1), :]
                level = lax.shift_right_logical(label, 7)
                value = conc_ref[pl.ds(r, species, stride=rows), :]
                high = value.astype(bf16).astype(f32)
                low = value - high
                picks.append(one_hot(label))
                here = [level == n for n in range(LEVELS)]
                blocks = [jnp.where(here[n], high, 0.0) for n in range(LEVELS)]
                blocks += [jnp.where(here[n], low, 0.0) for n in range(LEVELS)]
                blocks.append(jnp.where(iota((LEVELS, LANES), 0) == level, 1.0, 0.0))
                values.append(jnp.concatenate(blocks, axis=0).astype(bf16))
            jacc[...] += lax.dot_general(
                jnp.concatenate(values, axis=1), jnp.concatenate(picks, axis=1),
                (((1,), (1,)), ((), ())), preferred_element_type=f32,
            )
            return acc

        lax.fori_loop(first // ROWS_AT_ONCE, last // ROWS_AT_ONCE, body, 0)

    def look_up(table, labels):
        pick = jnp.concatenate([one_hot(label) for label in labels], axis=1)
        found = dot(table, pick)
        half = LEVELS * species
        results = []
        for t, label in enumerate(labels):
            level = lax.shift_right_logical(label, 7)
            column = found[:, t * LANES : (t + 1) * LANES]
            result = jnp.zeros((species, LANES), f32)
            for n in range(LEVELS):
                both = column[n * species : (n + 1) * species] + column[half + n * species : half + (n + 1) * species]
                result = result + jnp.where(level == n, both, 0.0)
            results.append(result)
        return results

    def means():
        half = LEVELS * species
        count = jnp.maximum(jacc[2 * half : 2 * half + LEVELS, :], 1.0)
        blocks = []
        for n in range(LEVELS):
            here = slice(n * species, (n + 1) * species)
            there = slice(half + n * species, half + (n + 1) * species)
            blocks.append((jacc[here, :] + jacc[there, :]) / count[n : n + 1])
        jmean[...] = jnp.concatenate(blocks, axis=0).reshape(jmean.shape)
        spread(lambda p: jmean.at[p], jrecv, SEM_J, "chan")

    def means_chan():
        arrived(jrecv, SEM_J)
        jsum[...] = jnp.sum(jrecv[...], axis=0)
        spread(lambda p: jsum, jwide, SEM_J + 1, "wide")

    def means_wide():
        arrived(jwide, SEM_J + 1)
        jpiece[...] = jnp.sum(jwide[...], axis=0)
        spread(lambda p: jpiece, jall, SEM_J + 2, "chan")

    def junction_table():
        arrived(jall, SEM_J + 2)
        table = jall[...].reshape(LEVELS * species, LANES)
        both = jnp.concatenate(split(table), axis=0)
        blocks = []
        for n in range(0, LEVELS, 2):
            found = look_up(both, [par_ref[n : n + 1, :], par_ref[n + 1 : n + 2, :]])
            for t in range(2):
                here = slice((n + t) * species, (n + t + 1) * species)
                blocks.append(coupling * (found[t] - table[here]))
        jtab[...] = jnp.concatenate(split(jnp.concatenate(blocks, axis=0)), axis=0)

    def source_rows(first, last):
        def body(i, acc):
            labels = [own_ref[pl.ds(i * ROWS_AT_ONCE + t, 1), :] for t in range(ROWS_AT_ONCE)]
            for t, found in enumerate(look_up(jtab[...], labels)):
                src[pl.ds(i * ROWS_AT_ONCE + t, species, stride=rows), :] = found
            return acc

        lax.fori_loop(first // ROWS_AT_ONCE, last // ROWS_AT_ONCE, body, 0)

    def conc_near(s):
        c = conc_ref[pl.ds(s * rows, rows), :]
        plane_l = jnp.where(wall_xl, c[:nz], conc_in[0, s])
        plane_r = jnp.where(wall_xr, c[rows - nz :], conc_in[1, s])
        line = cols_in[0, pl.ds(s + 2, 1), :], cols_in[1, pl.ds(s + 2, 1), :]
        sides = [jnp.broadcast_to(one, (cy, rows)).T for one in line]
        col_l = jnp.where(wall_yl, c, sides[0])
        col_r = jnp.where(wall_yr, c, sides[1])
        return c, neighbours(c, plane_l, plane_r, col_l, col_r, None)

    def start_species():
        arrived(conc_in.at[1], SEM_H + 6)
        arrived(conc_in.at[0], SEM_H + 7)
        for s in range(species):
            c, near_c = conc_near(s)
            flow = near_c[0]
            for k in range(1, 6):
                flow = flow + near_c[k]
            here = pl.ds(s * rows, rows)
            src[here, :] = src[here, :] + (4.0 * c - prev_ref[here, :]) + dif[s] * flow

    quarter = rows // 4
    jacc[...] = jnp.zeros_like(jacc)

    def fill(sweep, spot):
        if sweep == 0:
            if spot == 1:
                for copy in conc_halo:
                    copy.start()
            sum_rows((0, quarter, 2 * quarter)[spot], (quarter, 2 * quarter, 3 * quarter)[spot])
        elif sweep == 1:
            if spot == 0:
                sum_rows(3 * quarter, rows)
                means()
            elif spot == 1:
                means_chan()
            else:
                means_wide()
        elif sweep == 2:
            if spot == 0:
                junction_table()
            elif spot == 1:
                source_rows(0, quarter)
            else:
                source_rows(quarter, 2 * quarter)
        else:
            if spot == 0:
                source_rows(2 * quarter, 3 * quarter)
            elif spot == 1:
                source_rows(3 * quarter, rows)
            else:
                start_species()

    pick_row = iota((8, 2 * cy), 0)
    pick_lane = iota((8, 2 * cy), 1)
    pick = jnp.where(
        ((pick_row == 0) & (pick_lane < cy)) | ((pick_row == 1) & (pick_lane >= cy)), 1.0, 0.0
    ).astype(bf16)
    nt = (((1,), (1,)), ((), ()))

    for sweep in range(SWEEPS):
        field, near = phi_near(0)
        residual = charge[...]
        for k in range(6):
            residual = residual - faces[k] * (field - near[k])
        send1[sweep] = product((dt_h[...], dt_l[...]), residual).reshape(send1.shape[1:])
        spread(lambda p: send1.at[sweep, p], recv1.at[sweep], SEM_A + sweep, "chan")
        fill(sweep, 0)
        arrived(recv1.at[sweep], SEM_A + sweep)
        force = product((lt_h[...], lt_l[...]), recv1[sweep].reshape(modes, cy))
        high, low = split(jnp.concatenate([force * tab_p[...], force * tab_m[...]], axis=1))
        moments = lax.dot_general(pick, high, nt, preferred_element_type=f32)
        moments = moments + lax.dot_general(pick, low, nt, preferred_element_type=f32)
        send_g[sweep] = moments[0:2]
        spread(lambda p: send_g.at[sweep], recv_g.at[sweep], SEM_G + sweep, "wide")
        width = (wy_h[...], wy_l[...])
        inner = product_right(product_right(force, width) * tab_d[...], width)
        inner = product((lb_h[...], lb_l[...]), inner)
        fill(sweep, 1)
        arrived(recv_g.at[sweep], SEM_G + sweep)
        got = recv_g[sweep]
        ends = [jnp.sum(jnp.sum(got * coef[k], axis=0), axis=0, keepdims=True) for k in range(2)]
        back = lb_f[...]
        high, low = split(jnp.concatenate([back * ends[0], back * ends[1]], axis=1))
        outer = dot(high, edge_h[...]) + dot(low, edge_h[...]) + dot(high, edge_l[...])
        outer = jnp.concatenate([outer[:, :cy] + inner, outer[:, cy:]], axis=1)
        send2[sweep] = outer.reshape(send2.shape[1:])
        spread(lambda p: send2.at[sweep, p], recv2.at[sweep], SEM_B + sweep, "chan")
        fill(sweep, 2)
        arrived(recv2.at[sweep], SEM_B + sweep)
        phi_e[...] += product((db_h[...], db_l[...]), recv2[sweep].reshape(nc * (cx + 2) * nb, 2 * cy))

    field, near = phi_near(None)
    out_phi[...] = field
    drops = []
    for k in range(6):
        drop = field - near[k]
        if k == 0:
            drop = jnp.where((row < nz) & wall_xl, 0.0, drop)
        elif k == 1:
            drop = jnp.where((row >= rows - nz) & wall_xr, 0.0, drop)
        elif k == 4:
            drop = jnp.where(at_first & wall_yl, 0.0, drop)
        elif k == 5:
            drop = jnp.where(at_last & wall_yr, 0.0, drop)
        drops.append(drop)
    ups = [jnp.maximum(drop, 0.0) for drop in drops]
    downs = [jnp.maximum(-drop, 0.0) for drop in drops]
    up_all = ups[0] + ups[1] + ups[2] + ups[3] + ups[4] + ups[5]
    down_all = downs[0] + downs[1] + downs[2] + downs[3] + downs[4] + downs[5]
    for k in range(6):
        faces[k] = ups[k]
        faces[6 + k] = downs[k]
    for s in range(species):
        c, near_c = conc_near(s)
        drift = val[s] * dif[s]
        plus, minus = jnp.maximum(drift, 0.0), jnp.maximum(-drift, 0.0)
        top_part = src[pl.ds(s * rows, rows), :]
        for k in range(6):
            top_part = top_part + (plus * faces[6 + k] + minus * faces[k]) * near_c[k]
        out_conc[pl.ds(s * rows, rows), :] = top_part / ((3.0 + 6.0 * dif[s]) + plus * up_all + minus * down_all)

    for copy in halo:
        copy.wait_send()
    for k in (6, 7):
        pltpu.make_async_copy(conc_in.at[0], conc_in.at[0], send_sem.at[SEM_H + k]).wait()
    for sweep in range(SWEEPS):
        left(send1.at[sweep], SEM_A + sweep, nc - 1)
        left(recv_g.at[sweep], SEM_G + sweep, nw - 1)
        left(send2.at[sweep], SEM_B + sweep, nc - 1)
    left(jmean, SEM_J, nc - 1)
    left(jwide, SEM_J + 1, nw - 1)
    left(jall, SEM_J + 2, nc - 1)


def per_device(sizes, conc_now, conc_prev, phi_prev, owner, partner, valence, diffusivity):
    nc, nw = sizes
    species, cx, nz, cy = conc_now.shape
    nb = nz // nc
    rows, modes = cx * nz, nc * cx * nb
    t = make_tables(nc, cx, nz, cy)
    tables = [t["lam"], t["theta"], t["lam_y"], *t["depth_to"], *t["length_to"], *t["length_back"],
              t["length_back_f"], *t["depth_back"], *t["width"]]
    ext = (cx + 2) * nz
    jrow = LEVELS * species // nc
    vmem = pl.BlockSpec(memory_space=pltpu.VMEM)
    smem = pl.BlockSpec(memory_space=pltpu.SMEM)
    sems = 3 * SWEEPS + 8 + 3
    out_conc, out_phi = pl.pallas_call(
        functools.partial(kernel, (nc, nw, cx, nz, cy)),
        out_shape=(
            jax.ShapeDtypeStruct((species * rows, cy), f32),
            jax.ShapeDtypeStruct((rows, cy), f32),
        ),
        in_specs=[smem, smem] + [vmem] * (5 + len(tables)),
        out_specs=(vmem, vmem),
        scratch_shapes=[
            pltpu.VMEM((ext, 2 * cy), f32),
            pltpu.VMEM((12, rows, cy), f32),
            pltpu.VMEM((rows, cy), f32),
            pltpu.VMEM((modes, cy), f32),
            pltpu.VMEM((modes, cy), f32),
            pltpu.VMEM((modes, cy), f32),
            pltpu.VMEM((2 * modes, 2 * cy), bf16),
            pltpu.VMEM((2 * modes, 2 * cy), bf16),
            pltpu.VMEM((2, nw, 2, modes), f32),
            pltpu.VMEM((SWEEPS, nc, cx * nb, cy), f32),
            pltpu.VMEM((SWEEPS, nc, cx * nb, cy), f32),
            pltpu.VMEM((SWEEPS, 2, modes), f32),
            pltpu.VMEM((SWEEPS, nw, 2, modes), f32),
            pltpu.VMEM((SWEEPS, nc, (cx + 2) * nb, 2 * cy), f32),
            pltpu.VMEM((SWEEPS, nc, (cx + 2) * nb, 2 * cy), f32),
            pltpu.VMEM((rows, cy), f32),
            pltpu.VMEM((2 * LEVELS, rows), f32),
            pltpu.VMEM((2, LEVELS, rows), f32),
            pltpu.VMEM((2, 2, nz, cy), f32),
            pltpu.VMEM((2, species, nz, cy), f32),
            pltpu.VMEM((LEVELS * (2 * species + 1), LANES), f32),
            pltpu.VMEM((nc, jrow, LANES), f32),
            pltpu.VMEM((nc, jrow, LANES), f32),
            pltpu.VMEM((jrow, LANES), f32),
            pltpu.VMEM((nw, jrow, LANES), f32),
            pltpu.VMEM((jrow, LANES), f32),
            pltpu.VMEM((nc, jrow, LANES), f32),
            pltpu.VMEM((2 * LEVELS * species, LANES), bf16),
            pltpu.VMEM((species * rows, cy), f32),
            pltpu.SemaphoreType.DMA((sems,)),
            pltpu.SemaphoreType.DMA((sems,)),
        ],
        compiler_params=pltpu.CompilerParams(
            collective_id=0, has_side_effects=True, vmem_limit_bytes=48 * 1024 * 1024
        ),
        name="step",
    )(
        valence,
        diffusivity,
        conc_now.reshape(species * rows, cy),
        conc_prev.reshape(species * rows, cy),
        phi_prev.reshape(rows, cy),
        owner.reshape(rows, cy),
        partner.reshape(LEVELS, LANES),
        *[jnp.asarray(one) for one in tables],
    )
    return out_conc.reshape(conc_now.shape), out_phi.reshape(phi_prev.shape)


def solution(mesh):
    return jax.shard_map(
        functools.partial(per_device, (mesh.shape["chan"], mesh.shape["wide"])),
        mesh=mesh,
        in_specs=(
            P(None, "chan", None, "wide"),
            P(None, "chan", None, "wide"),
            P("chan", None, "wide"),
            P("chan", None, "wide"),
            P(),
            P(),
            P(),
        ),
        out_specs=(P(None, "chan", None, "wide"), P("chan", None, "wide")),
        check_vma=False,
    )
```

time: 899 us -> 100 us (0.11); the launches traced: 883 us -> 99.1 us
  other arithmetic: 251 us -> 0 us
  starting transfers between devices: 160 us -> 0 us
  matrix products: 142 us -> 0 us
  local copies, waits for them, and re-layouts: 132 us -> 16.2 us
  blocking collectives: 109 us -> 0 us
  Pallas kernels: 0 us -> 82.2 us
  waiting for transfers between devices: 73.7 us -> 0 us
  between operations: 16 us -> 0.7 us
    scatter-add x2 -> x0, other arithmetic: 222 us -> none  [the longest x1 112 us: per_device(): jax.ops.segment_sum(cell_rows, owners, num_segments=junction_total + 1)]
    dot_general x16 -> x0, matrix products: 138 us -> none  [the longest x4 67.5 us: per_device(): across = jnp.einsum('xzy,yb->xzb', spectrum, table_y, precision=highest)]
    all_to_all x13 -> x0, starting transfers between devices: 83 us -> none  [the longest x4 36.4 us: per_device(): lax.all_to_all(across, 'chan', split_axis=2, concat_axis=0, tiled=True)]
    pallas_call x0 -> x1, Pallas kernels: none -> 82.2 us  [per_device(): pl.pallas_call(functools.partial(kernel, (nc, nw, cx, nz, cy)), out_shape...]
    ppermute x28 -> x0, starting transfers between devices: 77.4 us -> none  [the longest x14 50.2 us: with_halo(): lax.ppermute(tail, axis, [(i, (i + 1) % count) for i in range(ends)])]
    psum x1 -> x0, blocking collectives: 75.3 us -> none  [per_device(): lax.psum((junction_sums, cell_counts), ('chan', 'wide'))]
    all_to_all x13 -> x0, waiting for transfers between devices: 64.4 us -> none  [the longest x4 24.8 us: per_device(): lax.all_to_all(across, 'chan', split_axis=2, concat_axis=0, tiled=True)]
    gather x2 -> x0, local copies, waits for them, and re-layouts: 62.1 us -> none  [the longest x1 54.5 us: per_device(): source = table[owners].T.reshape(concs.shape)]
  transfers between devices with their start and end apart: 42 -> 0, of which waited for: 18 -> 0; matrix products, arithmetic and copies ran while one was open for 45% -> 0% of each run, Pallas kernels for 0% -> 0%
where the time goes in v1:
time: 100 us; the launch traced here: 99.1 us
  Pallas kernels  82.2 us (82%)
  local copies, waits for them, and re-layouts  16.2 us (16%)
    pallas_call x1, Pallas kernels, per_device(): pl.pallas_call(functools.partial(kernel, (nc, nw, cx, nz, cy)), out_shape...  82.2 us
    unnamed x44, local copies, waits for them, and re-layouts  16.2 us

profile of v1, /device:TPU:1, one launch (start us, length us, event | category | flops | bytes accessed | tf_op | source)
XLA Modules:
  0.0 99.1 jit_solution(9163416675430505513)
XLA Ops:
  0.6 0.0 copy-start.9
  0.6 0.0 copy-start.18
  0.7 0.0 copy-start.19
  0.7 0.0 copy-start.20
  0.7 0.7 copy-done.9
  1.4 0.0 copy-done.18
  1.4 0.0 copy-done.19
  1.4 0.0 copy-done.20
  1.4 0.0 copy-start
  1.4 1.0 %copy-done = f32[8,2,64,128]{3,2,1,0:T(8,128)S(1)} copy-done((f32[8,2,64,128]{3,2,1,0:T(8,128)S(1)}, f32[8,2,64,128]{3,2,1,0:T(8,128)}, u32[]{:S(2)}) %copy-start) | copy-done | bytes 524312
  2.4 0.0 copy-start.1
  2.4 1.0 %copy-done.1 = f32[8,2,64,128]{3,2,1,0:T(8,128)S(1)} copy-done((f32[8,2,64,128]{3,2,1,0:T(8,128)S(1)}, f32[8,2,64,128]{3,2,1,0:T(8,128)}, u32[]{:S(2)}) %copy-start.1) | copy-done | bytes 524312
  3.5 0.0 copy-start.2
  3.5 0.9 copy-done.2
  4.4 0.0 copy-start.3
  4.4 0.9 copy-done.3
  5.3 0.0 copy-start.4
  5.3 0.9 copy-done.4
  6.2 0.0 copy-start.5
  6.2 0.8 copy-done.5
  7.0 0.0 copy-start.6
  7.0 0.8 copy-done.6
  7.9 0.0 copy-start.7
  7.9 0.8 copy-done.7
  8.7 0.0 copy-start.8
  8.7 0.8 copy-done.8
  9.6 0.0 copy-start.10
  9.6 0.8 copy-done.10
  10.3 0.0 copy-start.11
  10.3 0.8 copy-done.11
  11.1 0.0 copy-start.12
  11.1 0.8 copy-done.12
  11.8 0.0 copy-start.13
  11.8 0.8 copy-done.13
  12.6 0.0 copy-start.14
  12.6 0.8 copy-done.14
  13.4 0.0 copy-start.15
  13.4 0.7 copy-done.15
  14.1 0.0 copy-start.16
  14.1 0.7 copy-done.16
  14.8 0.0 copy-start.17
  14.8 0.7 copy-done.17
  15.5 82.2 %step.1 = (f32[1024,128]{1,0:T(8,128)S(1)}, f32[128,128]{1,0:T(8,128)S(1)}) custom-call(s32[8]{0:T(128)S(1)} %copy-done.18, f32[8]{0:T(128)S(1)} %copy-done.19, f32[1024,128]{1,0:T(8,128)S(1)} %bitcast.8, f32[1024,128]{1,0:T(8,128)S(1)} %bitcast.9, f32[128,128]{1,0:T(8,128)S(1)} %bitcast.10, s32[128,128]{1,0:T(8,128)S(1)} %bitcast.11, ...), custom_call_target="tpu_custom_call" | custom-call | tf_op jit(solution)/shard_map/step/pallas_call | solution.py:525
  97.7 0.8 copy.25
  98.5 0.6 copy.26
Async XLA Ops:
  0.6 0.8 copy-start.9
  0.6 0.8 copy-start.18
  0.7 0.7 copy-start.19
  0.7 0.7 copy-start.20
  1.4 1.0 %copy-start = (f32[8,2,64,128]{3,2,1,0:T(8,128)S(1)}, f32[8,2,64,128]{3,2,1,0:T(8,128)}, u32[]{:S(2)}) copy-start(f32[8,2,64,128]{3,2,1,0:T(8,128)} %param.21) | copy-start | bytes 1572868
  2.4 1.0 %copy-start.1 = (f32[8,2,64,128]{3,2,1,0:T(8,128)S(1)}, f32[8,2,64,128]{3,2,1,0:T(8,128)}, u32[]{:S(2)}) copy-start(f32[8,2,64,128]{3,2,1,0:T(8,128)} %param.22) | copy-start | bytes 1572868
  3.5 0.9 copy-start.2
  4.4 0.9 copy-start.3
  5.3 0.9 copy-start.4
  6.2 0.8 copy-start.5
  7.0 0.8 copy-start.6
  7.9 0.8 copy-start.7
  8.7 0.8 copy-start.8
  9.6 0.8 copy-start.10
  10.3 0.8 copy-start.11
  11.1 0.8 copy-start.12
  11.8 0.8 copy-start.13
  12.6 0.8 copy-start.14
  13.4 0.7 copy-start.15
  14.1 0.7 copy-start.16
  14.8 0.7 copy-start.17

commit v2 on v1

--- a/solution.py
+++ b/solution.py
@@ -53,21 +53,38 @@
     depth_back = np.zeros((cx + 2, nz, nc, cx + 2, nb))
     for xx in range(cx + 2):
         depth_back[xx, :, :, xx, :] = qz.reshape(nz, nc, nb)
+    depth_ring = np.zeros((cx, nz, cx, nb, nc))
+    for x in range(cx):
+        depth_ring[x, :, x, :, :] = qz.reshape(nz, nc, nb).transpose(0, 2, 1)
+    length_ring = np.zeros((nc, cx, nx, nb))
+    length_ring[:] = qx.reshape(nc, cx, nx)[..., None]
     modes = nx * nb
     lam = eigen_values(nx)[:, None] + eigen_values(nz)[None, :]
     lam = lam.reshape(nx, nc, nb).transpose(1, 0, 2).reshape(nc, 1, modes)
     theta = np.arccosh(1.0 + lam / 2.0)
-    return dict(
-        depth_to=halves(depth_to.reshape(nc * cx * nb, cx * nz)),
-        length_to=halves(length_to.reshape(modes, modes)),
-        length_back=halves(length_back.reshape(nc * (cx + 2) * nb, modes)),
-        length_back_f=np.asarray(length_back.reshape(nc * (cx + 2) * nb, modes), np.float32),
-        depth_back=halves(depth_back.reshape((cx + 2) * nz, nc * (cx + 2) * nb)),
-        width=halves(qy),
-        lam=np.asarray(lam, np.float32),
-        theta=np.asarray(theta, np.float32),
-        lam_y=np.asarray(eigen_values(cy)[None, :], np.float32),
+    big = dict(
+        dt=depth_to.reshape(nc * cx * nb, cx * nz),
+        lt=length_to.reshape(modes, modes),
+        lb=length_back.reshape(nc * (cx + 2) * nb, modes),
+        db=depth_back.reshape((cx + 2) * nz, nc * (cx + 2) * nb),
+        wy=qy,
+        dr=depth_ring.reshape(cx * nz, cx * nb * nc),
+        lr=length_ring.reshape(nc, cx * modes),
     )
+    places, parts, row = {}, [], 0
+    for name, table in big.items():
+        for k, half in enumerate(halves(table)):
+            height = -(-half.shape[0] // 32) * 32
+            block = np.zeros((height, 2 * LANES), bf16)
+            block[: half.shape[0], : half.shape[1]] = half
+            parts.append(block)
+            places[name, k] = (row, *half.shape)
+            row += height
+    small = np.zeros((nc, 8, max(modes, LANES)), np.float32)
+    small[:, 0, :modes] = theta[:, 0]
+    small[:, 1, :modes] = lam[:, 0]
+    small[:, 2, :cy] = eigen_values(cy)
+    return places, np.concatenate(parts, axis=0), small
 
 
 def dot(a, b):
@@ -94,16 +111,15 @@
 
 
 def kernel(
-    cfg,
-    val_ref, dif_ref, conc_ref, prev_ref, phi_ref, own_ref, par_ref,
-    lam_ref, theta_ref, lam_y_ref,
-    dt_h, dt_l, lt_h, lt_l, lb_h, lb_l, lb_f, db_h, db_l, wy_h, wy_l,
+    cfg, places,
+    val_hbm, dif_hbm, conc_hbm, prev_hbm, phi_hbm, own_hbm, par_hbm, big_hbm, small_hbm,
     out_conc, out_phi,
+    val_ref, dif_ref, conc_ref, prev_ref, phi_ref, own_ref, par_ref, big, small,
     phi_e, faces, charge, tab_p, tab_m, tab_d, edge_h, edge_l, coef,
     send1, recv1, send_g, recv_g, send2, recv2,
     sig, cols, cols_in, plane_in, conc_in,
     jacc, jmean, jrecv, jsum, jwide, jpiece, jall, jtab, src,
-    send_sem, recv_sem,
+    send_sem, recv_sem, load_sem,
 ):
     nc, nw, cx, nz, cy = cfg
     nb = nz // nc
@@ -125,8 +141,22 @@
         pl.semaphore_signal(barrier, inc=1, device_id={"wide": lax.rem(me_w + i, nw)}, device_id_type=MESH)
         return 0
 
+    loads = {}
+    for k, (name, there, here) in enumerate([
+        ("small", small_hbm.at[me_c], small), ("val", val_hbm, val_ref), ("dif", dif_hbm, dif_ref),
+        ("conc", conc_hbm, conc_ref), ("phi", phi_hbm, phi_ref), ("big", big_hbm, big),
+        ("own", own_hbm, own_ref), ("par", par_hbm, par_ref), ("prev", prev_hbm, prev_ref),
+    ]):
+        loads[name] = pltpu.make_async_copy(there, here, load_sem.at[k])
+        loads[name].start()
     lax.fori_loop(1, nc, greet_c, 0)
     lax.fori_loop(1, nw, greet_w, 0)
+
+    def table(name):
+        def half(k):
+            row, height, width = places[name, k]
+            return big[pl.ds(row, height), pl.ds(0, width)]
+        return half(0), half(1)
 
     lane = iota((rows, cy), 1)
     row = iota((rows, cy), 0)
@@ -134,6 +164,41 @@
     at_first, at_last = lane == 0, lane == cy - 1
     top, bottom = depth == 0, depth == nz - 1
 
+    loads["small"].wait()
+    theta_row = small[0:1, 0:modes]
+    theta = jnp.broadcast_to(theta_row, (cy, modes)).T
+    lam = jnp.broadcast_to(small[1:2, 0:modes], (cy, modes)).T
+    tab_d[...] = 1.0 / (lam + small[2:3, 0:cy])
+    place = iota((modes, cy), 1).astype(f32)
+    power = lambda n: jnp.exp(-theta * n)
+    tab_p[...] = power(place)
+    tab_m[...] = power(cy - 1.0 - place)
+    scale = 1.0 / (1.0 - power(2.0 * cy + 2.0))
+    edge_left = (power(place + 1.0) - power(2.0 * cy + 1.0 - place)) * scale
+    edge_right = (power(cy - place) - power(cy + 2.0 + place)) * scale
+    for k, edge in enumerate((edge_left, edge_right)):
+        high, low = split(edge)
+        here = pl.ds(k * modes, modes)
+        edge_h[here, pl.ds(0, cy)] = high
+        edge_l[here, pl.ds(0, cy)] = low
+    width1 = cy * nw + 1
+    rowp = lambda n: jnp.exp(-theta_row * n)
+    front = 1.0 / ((1.0 - rowp(2.0)) * (1.0 - rowp(2.0 * width1)))
+    for k in range(2):
+        at = (cy * me_w if k == 0 else cy * (me_w + 1) + 1).astype(f32)
+        below = (1.0 - rowp(2.0 * (width1 - at))) * front
+        above = (1.0 - rowp(2.0 * at)) * front
+        for w in range(nw):
+            lower = (w < me_w) if k == 0 else (w <= me_w)
+            n_plus = jnp.where(lower, at + (cy * w + 2.0), cy * w + 2.0 - at)
+            n_minus = jnp.where(lower, at - (cy * w + cy - 1.0), 2.0 * width1 - at - (cy * w + cy - 1.0))
+            factor = jnp.where(lower, below, above)
+            sign = jnp.where(lower, -1.0, 1.0)
+            coef[k, w, 0:1, :] = sign * factor * rowp(n_plus)
+            coef[k, w, 1:2, :] = -sign * factor * rowp(n_minus)
+
+    for name in ("val", "dif", "conc"):
+        loads[name].wait()
     val = [val_ref[s].astype(f32) for s in range(species)]
     dif = [dif_ref[s] for s in range(species)]
     total = jnp.zeros((rows, cy), f32)
@@ -148,6 +213,7 @@
     sigma = 1.0 + part / jnp.full((1, 1), weight_all, f32)
     sig[...] = sigma
     charge[...] = charge_scale * total
+    loads["phi"].wait()
     phi = phi_ref[...]
 
     packed = jnp.zeros((rows, cy), f32)
@@ -186,6 +252,18 @@
     for copy in halo:
         copy.start()
 
+    if nc == 32:
+        order = [(dx, dy, dc) for dx in range(4) for dy in range(4) for dc in range(2)]
+        hops = (0, 1, 2, 1)
+        order = sorted(order[1:], key=lambda o: -(hops[o[0]] + hops[o[1]]))
+        at_x = [lax.rem(me_c // 8 + d, 4) * 8 for d in range(4)]
+        at_y = [lax.rem(me_c // 2 + d, 4) * 2 for d in range(4)]
+        at_core = [lax.rem(me_c + d, 2) for d in range(2)]
+        peers_c = [at_x[dx] + at_y[dy] + at_core[dc] for dx, dy, dc in order]
+    else:
+        peers_c = [lax.rem(me_c + d, nc) for d in range(1, nc)]
+    peers_w = [lax.rem(me_w + d, nw) for d in sorted(range(1, nw), key=lambda d: -min(d, nw - d))]
+
     def spread(src, dst, k, axis):
         n, me = (nc, me_c) if axis == "chan" else (nw, me_w)
 
@@ -197,47 +275,18 @@
         lax.fori_loop(1, n, body, 0)
         pltpu.make_async_copy(src(me), dst.at[me], recv_sem.at[k]).start()
 
+    def spread_fast(src, dst, k, axis):
+        peers, me = (peers_c, me_c) if axis == "chan" else (peers_w, me_w)
+        for p in peers:
+            remote(src(p), dst.at[me], k, axis, p).start()
+        pltpu.make_async_copy(src(me), dst.at[me], recv_sem.at[k]).start()
+
     def arrived(dst, k):
         pltpu.make_async_copy(dst, dst, recv_sem.at[k]).wait()
 
     def left(ref, k, n):
         part_of = ref.at[pl.ds(0, n)]
         pltpu.make_async_copy(part_of, part_of, send_sem.at[k]).wait()
-
-    theta_row = theta_ref[me_c]
-    theta = jnp.broadcast_to(theta_row, (cy, modes)).T
-    lam = jnp.broadcast_to(lam_ref[me_c], (cy, modes)).T
-    tab_d[...] = 1.0 / (lam + lam_y_ref[...])
-    place = iota((modes, cy), 1).astype(f32)
-    power = lambda n: jnp.exp(-theta * n)
-    tab_p[...] = power(place)
-    tab_m[...] = power(cy - 1.0 - place)
-    scale = 1.0 / (1.0 - power(2.0 * cy + 2.0))
-    mlane = iota((modes, cy), 1)
-    edge_left = (power(place + 1.0) - power(2.0 * cy + 1.0 - place)) * scale
-    edge_right = (power(cy - place) - power(cy + 2.0 + place)) * scale
-    for k, edge in enumerate((edge_left, edge_right)):
-        high, low = split(edge)
-        here = pl.ds(k * modes, modes)
-        edge_h[here, pl.ds(0, cy)] = high
-        edge_l[here, pl.ds(0, cy)] = low
-        edge_h[here, pl.ds(cy, cy)] = jnp.where(mlane == (cy - 1 if k == 0 else 0), 1.0, 0.0).astype(bf16)
-        edge_l[here, pl.ds(cy, cy)] = jnp.zeros((modes, cy), bf16)
-    width1 = cy * nw + 1
-    rowp = lambda n: jnp.exp(-theta_row * n)
-    front = 1.0 / ((1.0 - rowp(2.0)) * (1.0 - rowp(2.0 * width1)))
-    for k in range(2):
-        at = (cy * me_w if k == 0 else cy * (me_w + 1) + 1).astype(f32)
-        below = (1.0 - rowp(2.0 * (width1 - at))) * front
-        above = (1.0 - rowp(2.0 * at)) * front
-        for w in range(nw):
-            lower = (w < me_w) if k == 0 else (w <= me_w)
-            n_plus = jnp.where(lower, at + (cy * w + 2.0), cy * w + 2.0 - at)
-            n_minus = jnp.where(lower, at - (cy * w + cy - 1.0), 2.0 * width1 - at - (cy * w + cy - 1.0))
-            factor = jnp.where(lower, below, above)
-            sign = jnp.where(lower, -1.0, 1.0)
-            coef[k, w, 0:1, :] = sign * factor * rowp(n_plus)
-            coef[k, w, 1:2, :] = -sign * factor * rowp(n_minus)
 
     for copy in halo:
         copy.wait_recv()
@@ -385,6 +434,7 @@
         return c, neighbours(c, plane_l, plane_r, col_l, col_r, None)
 
     def start_species():
+        loads["prev"].wait()
         arrived(conc_in.at[1], SEM_H + 6)
         arrived(conc_in.at[0], SEM_H + 7)
         for s in range(species):
@@ -403,6 +453,8 @@
             if spot == 1:
                 for copy in conc_halo:
                     copy.start()
+            if spot == 0:
+                loads["own"].wait()
             sum_rows((0, quarter, 2 * quarter)[spot], (quarter, 2 * quarter, 3 * quarter)[spot])
         elif sweep == 1:
             if spot == 0:
@@ -414,6 +466,7 @@
                 means_wide()
         elif sweep == 2:
             if spot == 0:
+                loads["par"].wait()
                 junction_table()
             elif spot == 1:
                 source_rows(0, quarter)
@@ -434,37 +487,55 @@
     ).astype(bf16)
     nt = (((1,), (1,)), ((), ()))
 
+    ring_row = iota((LANES, cx * modes), 0)
+    ring_at = iota((LANES, cx * modes), 1)
+    ring_pair = lax.rem((ring_row + 1) // 2, cy // 2)
+    ring_keep = (ring_pair == (ring_at // modes) * nb + lax.rem(ring_at, nb))
+    ring_left = lax.rem(ring_row, 2) == 1
+    loads["big"].wait()
+
     for sweep in range(SWEEPS):
         field, near = phi_near(0)
         residual = charge[...]
         for k in range(6):
             residual = residual - faces[k] * (field - near[k])
-        send1[sweep] = product((dt_h[...], dt_l[...]), residual).reshape(send1.shape[1:])
-        spread(lambda p: send1.at[sweep, p], recv1.at[sweep], SEM_A + sweep, "chan")
+        send1[sweep] = product(table("dt"), residual).reshape(send1.shape[1:])
+        spread_fast(lambda p: send1.at[sweep, p], recv1.at[sweep], SEM_A + sweep, "chan")
         fill(sweep, 0)
         arrived(recv1.at[sweep], SEM_A + sweep)
-        force = product((lt_h[...], lt_l[...]), recv1[sweep].reshape(modes, cy))
+        force = product(table("lt"), recv1[sweep].reshape(modes, cy))
         high, low = split(jnp.concatenate([force * tab_p[...], force * tab_m[...]], axis=1))
         moments = lax.dot_general(pick, high, nt, preferred_element_type=f32)
         moments = moments + lax.dot_general(pick, low, nt, preferred_element_type=f32)
         send_g[sweep] = moments[0:2]
-        spread(lambda p: send_g.at[sweep], recv_g.at[sweep], SEM_G + sweep, "wide")
-        width = (wy_h[...], wy_l[...])
+        spread_fast(lambda p: send_g.at[sweep], recv_g.at[sweep], SEM_G + sweep, "wide")
+        width = table("wy")
         inner = product_right(product_right(force, width) * tab_d[...], width)
-        inner = product((lb_h[...], lb_l[...]), inner)
+        inner = product(table("lb"), inner)
         fill(sweep, 1)
         arrived(recv_g.at[sweep], SEM_G + sweep)
         got = recv_g[sweep]
         ends = [jnp.sum(jnp.sum(got * coef[k], axis=0), axis=0, keepdims=True) for k in range(2)]
-        back = lb_f[...]
+        back_h, back_l = table("lb")
+        back = back_h.astype(f32) + back_l.astype(f32)
         high, low = split(jnp.concatenate([back * ends[0], back * ends[1]], axis=1))
-        outer = dot(high, edge_h[...]) + dot(low, edge_h[...]) + dot(high, edge_l[...])
-        outer = jnp.concatenate([outer[:, :cy] + inner, outer[:, cy:]], axis=1)
-        send2[sweep] = outer.reshape(send2.shape[1:])
-        spread(lambda p: send2.at[sweep, p], recv2.at[sweep], SEM_B + sweep, "chan")
+        outer = inner + dot(high, edge_h[...]) + dot(low, edge_h[...]) + dot(high, edge_l[...])
+        span = (cx + 2) * nb
+        send2[sweep, :, 0:span, :] = outer.reshape(nc, span, cy)
+        long_ends = [jnp.concatenate([one] * cx, axis=1) for one in ends]
+        high, low = split(jnp.where(ring_keep, jnp.where(ring_left, long_ends[0], long_ends[1]), 0.0))
+        ring_h, ring_l = table("lr")
+        ring = lax.dot_general(ring_h, high, nt, preferred_element_type=f32)
+        ring = ring + lax.dot_general(ring_h, low, nt, preferred_element_type=f32)
+        ring = ring + lax.dot_general(ring_l, high, nt, preferred_element_type=f32)
+        send2[sweep, :, span : span + 1, :] = ring.reshape(nc, 1, cy)
+        spread_fast(lambda p: send2.at[sweep, p], recv2.at[sweep], SEM_B + sweep, "chan")
         fill(sweep, 2)
         arrived(recv2.at[sweep], SEM_B + sweep)
-        phi_e[...] += product((db_h[...], db_l[...]), recv2[sweep].reshape(nc * (cx + 2) * nb, 2 * cy))
+        phi_e[:, 0:cy] += product(table("db"), recv2[sweep, :, 0:span, :].reshape(nc * span, cy))
+        ring = recv2[sweep, :, span : span + 1, :].reshape(nc, cy)
+        pieces = [pltpu.roll(ring, cy - 2 * j, 1) if j else ring for j in range(cx * nb)]
+        phi_e[nz : nz + rows, cy : 2 * cy] += product(table("dr"), jnp.concatenate(pieces, axis=0))
 
     field, near = phi_near(None)
     out_phi[...] = field
@@ -514,38 +585,46 @@
     species, cx, nz, cy = conc_now.shape
     nb = nz // nc
     rows, modes = cx * nz, nc * cx * nb
-    t = make_tables(nc, cx, nz, cy)
-    tables = [t["lam"], t["theta"], t["lam_y"], *t["depth_to"], *t["length_to"], *t["length_back"],
-              t["length_back_f"], *t["depth_back"], *t["width"]]
+    places, big, small = make_tables(nc, cx, nz, cy)
     ext = (cx + 2) * nz
     jrow = LEVELS * species // nc
     vmem = pl.BlockSpec(memory_space=pltpu.VMEM)
-    smem = pl.BlockSpec(memory_space=pltpu.SMEM)
+    hbm = pl.BlockSpec(memory_space=pltpu.HBM)
     sems = 3 * SWEEPS + 8 + 3
+    fix = lambda x: pltpu.with_memory_space_constraint(x, pltpu.HBM)
     out_conc, out_phi = pl.pallas_call(
-        functools.partial(kernel, (nc, nw, cx, nz, cy)),
+        functools.partial(kernel, (nc, nw, cx, nz, cy), places),
         out_shape=(
             jax.ShapeDtypeStruct((species * rows, cy), f32),
             jax.ShapeDtypeStruct((rows, cy), f32),
         ),
-        in_specs=[smem, smem] + [vmem] * (5 + len(tables)),
+        in_specs=[hbm] * 9,
         out_specs=(vmem, vmem),
         scratch_shapes=[
+            pltpu.SMEM((species,), jnp.int32),
+            pltpu.SMEM((species,), f32),
+            pltpu.VMEM((species * rows, cy), f32),
+            pltpu.VMEM((species * rows, cy), f32),
+            pltpu.VMEM((rows, cy), f32),
+            pltpu.VMEM((rows, cy), jnp.int32),
+            pltpu.VMEM((LEVELS, LANES), jnp.int32),
+            pltpu.VMEM(big.shape, bf16),
+            pltpu.VMEM(small.shape[1:], f32),
             pltpu.VMEM((ext, 2 * cy), f32),
             pltpu.VMEM((12, rows, cy), f32),
             pltpu.VMEM((rows, cy), f32),
             pltpu.VMEM((modes, cy), f32),
             pltpu.VMEM((modes, cy), f32),
             pltpu.VMEM((modes, cy), f32),
-            pltpu.VMEM((2 * modes, 2 * cy), bf16),
-            pltpu.VMEM((2 * modes, 2 * cy), bf16),
+            pltpu.VMEM((2 * modes, cy), bf16),
+            pltpu.VMEM((2 * modes, cy), bf16),
             pltpu.VMEM((2, nw, 2, modes), f32),
             pltpu.VMEM((SWEEPS, nc, cx * nb, cy), f32),
             pltpu.VMEM((SWEEPS, nc, cx * nb, cy), f32),
             pltpu.VMEM((SWEEPS, 2, modes), f32),
             pltpu.VMEM((SWEEPS, nw, 2, modes), f32),
-            pltpu.VMEM((SWEEPS, nc, (cx + 2) * nb, 2 * cy), f32),
-            pltpu.VMEM((SWEEPS, nc, (cx + 2) * nb, 2 * cy), f32),
+            pltpu.VMEM((SWEEPS, nc, (cx + 2) * nb + 1, cy), f32),
+            pltpu.VMEM((SWEEPS, nc, (cx + 2) * nb + 1, cy), f32),
             pltpu.VMEM((rows, cy), f32),
             pltpu.VMEM((2 * LEVELS, rows), f32),
             pltpu.VMEM((2, LEVELS, rows), f32),
@@ -562,20 +641,14 @@
             pltpu.VMEM((species * rows, cy), f32),
             pltpu.SemaphoreType.DMA((sems,)),
             pltpu.SemaphoreType.DMA((sems,)),
+            pltpu.SemaphoreType.DMA((9,)),
         ],
         compiler_params=pltpu.CompilerParams(
             collective_id=0, has_side_effects=True, vmem_limit_bytes=48 * 1024 * 1024
         ),
         name="step",
     )(
-        valence,
-        diffusivity,
-        conc_now.reshape(species * rows, cy),
-        conc_prev.reshape(species * rows, cy),
-        phi_prev.reshape(rows, cy),
-        owner.reshape(rows, cy),
-        partner.reshape(LEVELS, LANES),
-        *[jnp.asarray(one) for one in tables],
+        *[fix(x) for x in (valence, diffusivity, conc_now.reshape(species * rows, cy), conc_prev.reshape(species * rows, cy), phi_prev.reshape(rows, cy), owner.reshape(rows, cy), partner.reshape(LEVELS, LANES), jnp.asarray(big), jnp.asarray(small))]
     )
     return out_conc.reshape(conc_now.shape), out_phi.reshape(phi_prev.shape)
 

time: 100 us -> 79.1 us (0.79)
  local copies, waits for them, and re-layouts: 16.2 us -> 1.42 us
  Pallas kernels: 82.2 us -> 76.9 us
    unnamed x44 -> x2, local copies, waits for them, and re-layouts: 16.2 us -> 1.42 us
    pallas_call x1, Pallas kernels: 82.2 us -> 76.9 us  [per_device(): pl.pallas_call(functools.partial(kernel, (nc, nw, cx, nz, cy), places), o...]
where the time goes in v2:
time: 79.1 us; the launch traced here: 79 us
  Pallas kernels  76.9 us (97%)
  local copies, waits for them, and re-layouts  1.42 us (2%)
    pallas_call x1, Pallas kernels, per_device(): pl.pallas_call(functools.partial(kernel, (nc, nw, cx, nz, cy), places), o...  76.9 us

profile of v2, /device:TPU:1, one launch (start us, length us, event | category | flops | bytes accessed | tf_op | source)
XLA Modules:
  0.0 79.0 jit_solution(17347083134691680282)
XLA Ops:
  0.6 76.9 %step.1 = (f32[1024,128]{1,0:T(8,128)S(1)}, f32[128,128]{1,0:T(8,128)S(1)}) custom-call(s32[8]{0:T(128)} %val_hbm.1, f32[8]{0:T(128)} %dif_hbm.1, f32[1024,128]{1,0:T(8,128)} %bitcast.9, f32[1024,128]{1,0:T(8,128)} %bitcast.10, f32[128,128]{1,0:T(8,128)} %bitcast.11, s32[128,128]{1,0:T(8,128)} %bitcast.12, s32[16,128]{1,0:T(8,128)} %bitcast.13, ...), custom_call_target="tpu_custom_call" | custom-call | tf_op jit(solution)/shard_map/step/pallas_call | solution.py:595
  77.6 0.8 %copy.13 = f32[8,2,64,128]{3,2,1,0:T(8,128)} copy(f32[8,2,64,128]{3,2,1,0:T(8,128)S(1)} %bitcast.7) | data formatting | bytes 1048576
  78.4 0.6 copy.14

commit v3 on v2

--- a/solution.py
+++ b/solution.py
@@ -115,11 +115,11 @@
     val_hbm, dif_hbm, conc_hbm, prev_hbm, phi_hbm, own_hbm, par_hbm, big_hbm, small_hbm,
     out_conc, out_phi,
     val_ref, dif_ref, conc_ref, prev_ref, phi_ref, own_ref, par_ref, big, small,
-    phi_e, faces, charge, tab_p, tab_m, tab_d, edge_h, edge_l, coef,
+    phi_e, faces, flows, beside, columns, charge, tab_p, tab_m, tab_d, edge_h, edge_l, coef,
     send1, recv1, send_g, recv_g, send2, recv2,
     sig, cols, cols_in, plane_in, conc_in,
     jacc, jmean, jrecv, jsum, jwide, jpiece, jall, jtab, src,
-    send_sem, recv_sem, load_sem,
+    send_sem, recv_sem, load_sem, known,
 ):
     nc, nw, cx, nz, cy = cfg
     nb = nz // nc
@@ -133,24 +133,44 @@
 
     barrier = pltpu.get_barrier_semaphore()
 
-    def greet_c(i, _):
-        pl.semaphore_signal(barrier, inc=1, device_id={"chan": lax.rem(me_c + i, nc)}, device_id_type=MESH)
-        return 0
-
-    def greet_w(i, _):
-        pl.semaphore_signal(barrier, inc=1, device_id={"wide": lax.rem(me_w + i, nw)}, device_id_type=MESH)
-        return 0
+    if nc == 32:
+        order = [(dx, dy, dc) for dx in range(4) for dy in range(4) for dc in range(2)]
+        hops = (0, 1, 2, 1)
+        order = sorted(order[1:], key=lambda o: -(hops[o[0]] + hops[o[1]]))
+        at_x = [lax.rem(me_c // 8 + d, 4) * 8 for d in range(4)]
+        at_y = [lax.rem(me_c // 2 + d, 4) * 2 for d in range(4)]
+        at_core = [lax.rem(me_c + d, 2) for d in range(2)]
+        peers_c = [at_x[dx] + at_y[dy] + at_core[dc] for dx, dy, dc in order]
+    else:
+        peers_c = [lax.rem(me_c + d, nc) for d in range(1, nc)]
+    peers_w = [lax.rem(me_w + d, nw) for d in sorted(range(1, nw), key=lambda d: -min(d, nw - d))]
+
+    dx_all, dy_all = {32: (4, 4), 8: (2, 2), 4: (2, 1)}[nc]
+    core = lax.rem(me_c, 2)
+    chip_y = lax.rem(me_c // 2, dy_all)
+    chip_x = me_c // (2 * dy_all)
+    chip = lambda x, y, c: (x * dy_all + y) * 2 + c
+    partner_core = chip(chip_x, chip_y, 1 - core)
+    beside_chip = jnp.where(core == 0, left_c, right_c)
+    row_peers = [chip(lax.rem(chip_x + d, dx_all), chip_y, core) for d in range(1, dx_all)]
+    column_peers = [chip(chip_x, lax.rem(chip_y + d, dy_all), core) for d in range(1, dy_all)]
+    width_peers = [left_w, right_w] if nw > 2 else [right_w]
+
+    def tell(semaphore, axis, peers):
+        for p in peers:
+            pl.semaphore_signal(semaphore, inc=1, device_id={axis: p}, device_id_type=MESH)
+
+    tell(barrier, "wide", width_peers)
+    tell(barrier, "chan", [beside_chip] + row_peers + column_peers + [partner_core])
 
     loads = {}
     for k, (name, there, here) in enumerate([
-        ("small", small_hbm.at[me_c], small), ("val", val_hbm, val_ref), ("dif", dif_hbm, dif_ref),
-        ("conc", conc_hbm, conc_ref), ("phi", phi_hbm, phi_ref), ("big", big_hbm, big),
+        ("conc", conc_hbm, conc_ref), ("val", val_hbm, val_ref), ("dif", dif_hbm, dif_ref),
+        ("phi", phi_hbm, phi_ref), ("small", small_hbm.at[me_c], small), ("big", big_hbm, big),
         ("own", own_hbm, own_ref), ("par", par_hbm, par_ref), ("prev", prev_hbm, prev_ref),
     ]):
         loads[name] = pltpu.make_async_copy(there, here, load_sem.at[k])
         loads[name].start()
-    lax.fori_loop(1, nc, greet_c, 0)
-    lax.fori_loop(1, nw, greet_w, 0)
 
     def table(name):
         def half(k):
@@ -164,6 +184,96 @@
     at_first, at_last = lane == 0, lane == cy - 1
     top, bottom = depth == 0, depth == nz - 1
 
+    for name in ("val", "dif", "conc"):
+        loads[name].wait()
+    val = [val_ref[s].astype(f32) for s in range(species)]
+    dif = [dif_ref[s] for s in range(species)]
+    total = jnp.zeros((rows, cy), f32)
+    part = jnp.zeros((rows, cy), f32)
+    weight_all = jnp.float32(0.0)
+    for s in range(species):
+        c = conc_ref[pl.ds(s * rows, rows), :]
+        square = val[s] * val[s]
+        weight_all = weight_all + (square + 1.0) * dif[s]
+        part = part + (square * dif[s]) * c * c
+        total = total + val[s] * c
+    sigma = 1.0 + part / jnp.full((1, 1), weight_all, f32)
+    sig[...] = sigma
+    loads["phi"].wait()
+    phi = phi_ref[...]
+
+    packed = jnp.zeros((rows, cy), f32)
+    for k in range(species + 2):
+        field = phi if k == 0 else sigma if k == 1 else conc_ref[pl.ds((k - 2) * rows, rows), :]
+        packed = jnp.where(lane == k, pltpu.roll(field, k, 1) if k else field, packed)
+        packed = jnp.where(lane == LEVELS + k, pltpu.roll(field, LEVELS + 1 + k, 1), packed)
+    cols[...] = packed.T[: 2 * LEVELS]
+
+    pl.semaphore_wait(barrier, 2 + len(row_peers) + len(column_peers) + len(width_peers))
+
+    SEM_A, SEM_G, SEM_B = 0, SWEEPS, 2 * SWEEPS
+    SEM_H = 3 * SWEEPS
+    SEM_J = SEM_H + 8
+
+    def remote(src, dst, k, axis, place):
+        return pltpu.make_async_remote_copy(
+            src_ref=src, dst_ref=dst, send_sem=send_sem.at[k], recv_sem=recv_sem.at[k],
+            device_id={axis: place}, device_id_type=MESH,
+        )
+
+    halo = [
+        remote(cols.at[pl.ds(0, LEVELS)], cols_in.at[1], SEM_H, "wide", left_w),
+        remote(cols.at[pl.ds(LEVELS, LEVELS)], cols_in.at[0], SEM_H + 1, "wide", right_w),
+        remote(sig.at[pl.ds(0, nz)], plane_in.at[1, 0], SEM_H + 2, "chan", left_c),
+        remote(sig.at[pl.ds(rows - nz, nz)], plane_in.at[0, 0], SEM_H + 3, "chan", right_c),
+        remote(phi_ref.at[pl.ds(0, nz)], plane_in.at[1, 1], SEM_H + 4, "chan", left_c),
+        remote(phi_ref.at[pl.ds(rows - nz, nz)], plane_in.at[0, 1], SEM_H + 5, "chan", right_c),
+    ]
+    conc_halo = []
+    for s in range(species):
+        conc_halo += [
+            remote(conc_ref.at[pl.ds(s * rows, nz)], conc_in.at[1, s], SEM_H + 6, "chan", left_c),
+            remote(conc_ref.at[pl.ds((s + 1) * rows - nz, nz)], conc_in.at[0, s], SEM_H + 7, "chan", right_c),
+        ]
+    for copy in halo:
+        copy.start()
+
+    far_steps = nw // 2 - 1
+
+    def known_w(k):
+        if k > 0 and k <= far_steps:
+            pl.semaphore_wait(known.at[1 + k], len(width_peers))
+        if k < far_steps:
+            tell(known.at[2 + k], "wide", width_peers)
+
+    tell(known.at[0], "chan", row_peers)
+    known_w(0)
+
+    def spread(src, dst, k, axis):
+        n, me = (nc, me_c) if axis == "chan" else (nw, me_w)
+
+        def body(i, _):
+            p = lax.rem(me + i, n)
+            remote(src(p), dst.at[me], k, axis, p).start()
+            return 0
+
+        lax.fori_loop(1, n, body, 0)
+        pltpu.make_async_copy(src(me), dst.at[me], recv_sem.at[k]).start()
+
+    def spread_fast(src, dst, k, axis):
+        peers, me = (peers_c, me_c) if axis == "chan" else (peers_w, me_w)
+        for p in peers:
+            remote(src(p), dst.at[me], k, axis, p).start()
+        pltpu.make_async_copy(src(me), dst.at[me], recv_sem.at[k]).start()
+
+    def arrived(dst, k):
+        pltpu.make_async_copy(dst, dst, recv_sem.at[k]).wait()
+
+    def left(ref, k, n):
+        part_of = ref.at[pl.ds(0, n)]
+        pltpu.make_async_copy(part_of, part_of, send_sem.at[k]).wait()
+
+    charge[...] = charge_scale * total
     loads["small"].wait()
     theta_row = small[0:1, 0:modes]
     theta = jnp.broadcast_to(theta_row, (cy, modes)).T
@@ -197,99 +307,16 @@
             coef[k, w, 0:1, :] = sign * factor * rowp(n_plus)
             coef[k, w, 1:2, :] = -sign * factor * rowp(n_minus)
 
-    for name in ("val", "dif", "conc"):
-        loads[name].wait()
-    val = [val_ref[s].astype(f32) for s in range(species)]
-    dif = [dif_ref[s] for s in range(species)]
-    total = jnp.zeros((rows, cy), f32)
-    part = jnp.zeros((rows, cy), f32)
-    weight_all = jnp.float32(0.0)
-    for s in range(species):
-        c = conc_ref[pl.ds(s * rows, rows), :]
-        square = val[s] * val[s]
-        weight_all = weight_all + (square + 1.0) * dif[s]
-        part = part + (square * dif[s]) * c * c
-        total = total + val[s] * c
-    sigma = 1.0 + part / jnp.full((1, 1), weight_all, f32)
-    sig[...] = sigma
-    charge[...] = charge_scale * total
-    loads["phi"].wait()
-    phi = phi_ref[...]
-
-    packed = jnp.zeros((rows, cy), f32)
-    for k in range(species + 2):
-        field = phi if k == 0 else sigma if k == 1 else conc_ref[pl.ds((k - 2) * rows, rows), :]
-        packed = jnp.where(lane == k, pltpu.roll(field, k, 1) if k else field, packed)
-        packed = jnp.where(lane == LEVELS + k, pltpu.roll(field, LEVELS + 1 + k, 1), packed)
-    cols[...] = packed.T[: 2 * LEVELS]
-
-    pl.semaphore_wait(barrier, nc - 1 + nw - 1)
-
-    SEM_A, SEM_G, SEM_B = 0, SWEEPS, 2 * SWEEPS
-    SEM_H = 3 * SWEEPS
-    SEM_J = SEM_H + 8
-
-    def remote(src, dst, k, axis, place):
-        return pltpu.make_async_remote_copy(
-            src_ref=src, dst_ref=dst, send_sem=send_sem.at[k], recv_sem=recv_sem.at[k],
-            device_id={axis: place}, device_id_type=MESH,
-        )
-
-    halo = [
-        remote(cols.at[pl.ds(0, LEVELS)], cols_in.at[1], SEM_H, "wide", left_w),
-        remote(cols.at[pl.ds(LEVELS, LEVELS)], cols_in.at[0], SEM_H + 1, "wide", right_w),
-        remote(sig.at[pl.ds(0, nz)], plane_in.at[1, 0], SEM_H + 2, "chan", left_c),
-        remote(sig.at[pl.ds(rows - nz, nz)], plane_in.at[0, 0], SEM_H + 3, "chan", right_c),
-        remote(phi_ref.at[pl.ds(0, nz)], plane_in.at[1, 1], SEM_H + 4, "chan", left_c),
-        remote(phi_ref.at[pl.ds(rows - nz, nz)], plane_in.at[0, 1], SEM_H + 5, "chan", right_c),
-    ]
-    conc_halo = []
-    for s in range(species):
-        conc_halo += [
-            remote(conc_ref.at[pl.ds(s * rows, nz)], conc_in.at[1, s], SEM_H + 6, "chan", left_c),
-            remote(conc_ref.at[pl.ds((s + 1) * rows - nz, nz)], conc_in.at[0, s], SEM_H + 7, "chan", right_c),
-        ]
-    for copy in halo:
-        copy.start()
-
-    if nc == 32:
-        order = [(dx, dy, dc) for dx in range(4) for dy in range(4) for dc in range(2)]
-        hops = (0, 1, 2, 1)
-        order = sorted(order[1:], key=lambda o: -(hops[o[0]] + hops[o[1]]))
-        at_x = [lax.rem(me_c // 8 + d, 4) * 8 for d in range(4)]
-        at_y = [lax.rem(me_c // 2 + d, 4) * 2 for d in range(4)]
-        at_core = [lax.rem(me_c + d, 2) for d in range(2)]
-        peers_c = [at_x[dx] + at_y[dy] + at_core[dc] for dx, dy, dc in order]
-    else:
-        peers_c = [lax.rem(me_c + d, nc) for d in range(1, nc)]
-    peers_w = [lax.rem(me_w + d, nw) for d in sorted(range(1, nw), key=lambda d: -min(d, nw - d))]
-
-    def spread(src, dst, k, axis):
-        n, me = (nc, me_c) if axis == "chan" else (nw, me_w)
-
-        def body(i, _):
-            p = lax.rem(me + i, n)
-            remote(src(p), dst.at[me], k, axis, p).start()
-            return 0
-
-        lax.fori_loop(1, n, body, 0)
-        pltpu.make_async_copy(src(me), dst.at[me], recv_sem.at[k]).start()
-
-    def spread_fast(src, dst, k, axis):
-        peers, me = (peers_c, me_c) if axis == "chan" else (peers_w, me_w)
-        for p in peers:
-            remote(src(p), dst.at[me], k, axis, p).start()
-        pltpu.make_async_copy(src(me), dst.at[me], recv_sem.at[k]).start()
-
-    def arrived(dst, k):
-        pltpu.make_async_copy(dst, dst, recv_sem.at[k]).wait()
-
-    def left(ref, k, n):
-        part_of = ref.at[pl.ds(0, n)]
-        pltpu.make_async_copy(part_of, part_of, send_sem.at[k]).wait()
+    pl.semaphore_wait(known.at[0], len(row_peers))
+    tell(known.at[1], "chan", [partner_core])
+    known_w(1)
+    jacc[...] = jnp.zeros_like(jacc)
+    faces[2] = 0.5 * (sigma + jnp.where(top, 0.0, pltpu.roll(sigma, 1, 0)))
+    faces[3] = 0.5 * (sigma + jnp.where(bottom, 0.0, pltpu.roll(sigma, rows - 1, 0)))
 
     for copy in halo:
         copy.wait_recv()
+    known_w(2)
     wall_xl, wall_xr = me_c == 0, me_c == nc - 1
     wall_yl, wall_yr = me_w == 0, me_w == nw - 1
     keep_xl, keep_xr = jnp.where(wall_xl, 0.0, 1.0), jnp.where(wall_xr, 0.0, 1.0)
@@ -298,6 +325,7 @@
         [cols_in[0], cols_in[1], jnp.zeros((cy - 2 * LEVELS, rows), f32)], axis=0
     )
     col_in = stacked.T
+    columns[...] = col_in
 
     def neighbours(field, plane_l, plane_r, col_l, col_r, edge):
         low = field if edge is None else jnp.zeros_like(field)
@@ -314,7 +342,7 @@
         sigma, plane_in[0, 0] * keep_xl, plane_in[1, 0] * keep_xr,
         col_in[:, 1:2] * keep_yl, col_in[:, LEVELS + 1 : LEVELS + 2] * keep_yr, 0,
     )
-    for k in range(6):
+    for k in (0, 1, 4, 5):
         faces[k] = 0.5 * (sigma + near[k])
     phi_e[0:nz, 0:cy] = plane_in[0, 1] * keep_xl
     phi_e[nz : nz + rows, 0:cy] = phi
@@ -427,10 +455,8 @@
         c = conc_ref[pl.ds(s * rows, rows), :]
         plane_l = jnp.where(wall_xl, c[:nz], conc_in[0, s])
         plane_r = jnp.where(wall_xr, c[rows - nz :], conc_in[1, s])
-        line = cols_in[0, pl.ds(s + 2, 1), :], cols_in[1, pl.ds(s + 2, 1), :]
-        sides = [jnp.broadcast_to(one, (cy, rows)).T for one in line]
-        col_l = jnp.where(wall_yl, c, sides[0])
-        col_r = jnp.where(wall_yr, c, sides[1])
+        col_l = jnp.where(wall_yl, c, columns[:, s + 2 : s + 3])
+        col_r = jnp.where(wall_yr, c, columns[:, LEVELS + s + 2 : LEVELS + s + 3])
         return c, neighbours(c, plane_l, plane_r, col_l, col_r, None)
 
     def start_species():
@@ -440,13 +466,13 @@
         for s in range(species):
             c, near_c = conc_near(s)
             flow = near_c[0]
-            for k in range(1, 6):
-                flow = flow + near_c[k]
+            for k in range(6):
+                beside[s, k] = near_c[k]
+                flow = flow + near_c[k] if k else flow
             here = pl.ds(s * rows, rows)
             src[here, :] = src[here, :] + (4.0 * c - prev_ref[here, :]) + dif[s] * flow
 
     quarter = rows // 4
-    jacc[...] = jnp.zeros_like(jacc)
 
     def fill(sweep, spot):
         if sweep == 0:
@@ -493,6 +519,7 @@
     ring_keep = (ring_pair == (ring_at // modes) * nb + lax.rem(ring_at, nb))
     ring_left = lax.rem(ring_row, 2) == 1
     loads["big"].wait()
+    pl.semaphore_wait(known.at[1], 1)
 
     for sweep in range(SWEEPS):
         field, near = phi_near(0)
@@ -508,6 +535,9 @@
         moments = lax.dot_general(pick, high, nt, preferred_element_type=f32)
         moments = moments + lax.dot_general(pick, low, nt, preferred_element_type=f32)
         send_g[sweep] = moments[0:2]
+        if sweep == 0:
+            for k in range(3, far_steps + 1):
+                known_w(k)
         spread_fast(lambda p: send_g.at[sweep], recv_g.at[sweep], SEM_G + sweep, "wide")
         width = table("wy")
         inner = product_right(product_right(force, width) * tab_d[...], width)
@@ -551,21 +581,20 @@
         elif k == 5:
             drop = jnp.where(at_last & wall_yr, 0.0, drop)
         drops.append(drop)
-    ups = [jnp.maximum(drop, 0.0) for drop in drops]
-    downs = [jnp.maximum(-drop, 0.0) for drop in drops]
-    up_all = ups[0] + ups[1] + ups[2] + ups[3] + ups[4] + ups[5]
-    down_all = downs[0] + downs[1] + downs[2] + downs[3] + downs[4] + downs[5]
+    outs = [jnp.zeros((rows, cy), f32)] * 2
     for k in range(6):
-        faces[k] = ups[k]
-        faces[6 + k] = downs[k]
+        up, down = jnp.maximum(drops[k], 0.0), jnp.maximum(-drops[k], 0.0)
+        flows[0, k], flows[1, k] = down, up
+        outs = [outs[0] + up, outs[1] + down]
+    flows[0, 6], flows[1, 6] = outs
     for s in range(species):
-        c, near_c = conc_near(s)
-        drift = val[s] * dif[s]
-        plus, minus = jnp.maximum(drift, 0.0), jnp.maximum(-drift, 0.0)
-        top_part = src[pl.ds(s * rows, rows), :]
-        for k in range(6):
-            top_part = top_part + (plus * faces[6 + k] + minus * faces[k]) * near_c[k]
-        out_conc[pl.ds(s * rows, rows), :] = top_part / ((3.0 + 6.0 * dif[s]) + plus * up_all + minus * down_all)
+        sign = jnp.where(val_ref[s] < 0, 1, 0)
+        drift = jnp.abs(val[s] * dif[s])
+        inward = flows[sign, 0] * beside[s, 0]
+        for k in range(1, 6):
+            inward = inward + flows[sign, k] * beside[s, k]
+        here = pl.ds(s * rows, rows)
+        out_conc[here, :] = (src[here, :] + drift * inward) / ((3.0 + 6.0 * dif[s]) + drift * flows[sign, 6])
 
     for copy in halo:
         copy.wait_send()
@@ -611,7 +640,10 @@
             pltpu.VMEM(big.shape, bf16),
             pltpu.VMEM(small.shape[1:], f32),
             pltpu.VMEM((ext, 2 * cy), f32),
-            pltpu.VMEM((12, rows, cy), f32),
+            pltpu.VMEM((6, rows, cy), f32),
+            pltpu.VMEM((2, 7, rows, cy), f32),
+            pltpu.VMEM((species, 6, rows, cy), f32),
+            pltpu.VMEM((rows, cy), f32),
             pltpu.VMEM((rows, cy), f32),
             pltpu.VMEM((modes, cy), f32),
             pltpu.VMEM((modes, cy), f32),
@@ -642,6 +674,7 @@
             pltpu.SemaphoreType.DMA((sems,)),
             pltpu.SemaphoreType.DMA((sems,)),
             pltpu.SemaphoreType.DMA((9,)),
+            pltpu.SemaphoreType.REGULAR((2 + max(nw // 2 - 1, 1),)),
         ],
         compiler_params=pltpu.CompilerParams(
             collective_id=0, has_side_effects=True, vmem_limit_bytes=48 * 1024 * 1024

time: 79.1 us -> 77.1 us (0.975)
  Pallas kernels: 76.9 us -> 74.9 us
    pallas_call x1, Pallas kernels: 76.9 us -> 74.9 us  [per_device(): pl.pallas_call(functools.partial(kernel, (nc, nw, cx, nz, cy), places), o...]
where the time goes in v3:
time: 77.1 us; the launch traced here: 77 us
  Pallas kernels  74.9 us (97%)
  local copies, waits for them, and re-layouts  1.42 us (2%)
    pallas_call x1, Pallas kernels, per_device(): pl.pallas_call(functools.partial(kernel, (nc, nw, cx, nz, cy), places), o...  74.9 us

profile of v3, /device:TPU:1, one launch (start us, length us, event | category | flops | bytes accessed | tf_op | source)
XLA Modules:
  0.0 77.0 jit_solution(13544392529025489344)
XLA Ops:
  0.6 74.9 %step.1 = (f32[1024,128]{1,0:T(8,128)S(1)}, f32[128,128]{1,0:T(8,128)S(1)}) custom-call(s32[8]{0:T(128)} %val_hbm.1, f32[8]{0:T(128)} %dif_hbm.1, f32[1024,128]{1,0:T(8,128)} %bitcast.9, f32[1024,128]{1,0:T(8,128)} %bitcast.10, f32[128,128]{1,0:T(8,128)} %bitcast.11, s32[128,128]{1,0:T(8,128)} %bitcast.12, s32[16,128]{1,0:T(8,128)} %bitcast.13, ...), custom_call_target="tpu_custom_call" | custom-call | tf_op jit(solution)/shard_map/step/pallas_call | solution.py:624
  75.5 0.8 %copy.13 = f32[8,2,64,128]{3,2,1,0:T(8,128)} copy(f32[8,2,64,128]{3,2,1,0:T(8,128)S(1)} %bitcast.7) | data formatting | bytes 1048576
  76.3 0.6 copy.14

commit v4 on v3

--- a/solution.py
+++ b/solution.py
@@ -56,8 +56,13 @@
     depth_ring = np.zeros((cx, nz, cx, nb, nc))
     for x in range(cx):
         depth_ring[x, :, x, :, :] = qz.reshape(nz, nc, nb).transpose(0, 2, 1)
-    length_ring = np.zeros((nc, cx, nx, nb))
-    length_ring[:] = qx.reshape(nc, cx, nx)[..., None]
+    length_ring = np.zeros((cx, nc, nx, nb))
+    length_ring[:] = qx.reshape(nc, cx, nx).transpose(1, 0, 2)[..., None]
+    lane_pick = np.zeros((cx, 2, nx, nb, cy))
+    for x in range(cx):
+        for b in range(nb):
+            lane_pick[x, 0, :, b, (2 * (x * nb + b) - 1) % cy] = 1.0
+            lane_pick[x, 1, :, b, 2 * (x * nb + b)] = 1.0
     modes = nx * nb
     lam = eigen_values(nx)[:, None] + eigen_values(nz)[None, :]
     lam = lam.reshape(nx, nc, nb).transpose(1, 0, 2).reshape(nc, 1, modes)
@@ -69,11 +74,19 @@
         db=depth_back.reshape((cx + 2) * nz, nc * (cx + 2) * nb),
         wy=qy,
         dr=depth_ring.reshape(cx * nz, cx * nb * nc),
-        lr=length_ring.reshape(nc, cx * modes),
+        lr=length_ring.reshape(cx * nc, modes),
+        lp=lane_pick.reshape(cx * 2 * modes, cy),
     )
     places, parts, row = {}, [], 0
     for name, table in big.items():
-        for k, half in enumerate(halves(table)):
+        pair = halves(table)
+        if name in ("dt", "lt", "lb", "dr"):
+            pair = (np.concatenate(pair, axis=1),)
+        if name == "lr":
+            pair = (np.concatenate(pair, axis=0),)
+        if name == "lp":
+            pair = pair[:1]
+        for k, half in enumerate(pair):
             height = -(-half.shape[0] // 32) * 32
             block = np.zeros((height, 2 * LANES), bf16)
             block[: half.shape[0], : half.shape[1]] = half
@@ -98,7 +111,9 @@
 
 def product(table, value):
     high, low = split(value)
-    return dot(table[0], high) + dot(table[1], high) + dot(table[0], low)
+    width = value.shape[1]
+    found = dot(table[0], jnp.concatenate([high, low], axis=1))
+    return found[:, :width] + found[:, width:] + dot(table[1], high)
 
 
 def product_right(value, table):
@@ -115,7 +130,7 @@
     val_hbm, dif_hbm, conc_hbm, prev_hbm, phi_hbm, own_hbm, par_hbm, big_hbm, small_hbm,
     out_conc, out_phi,
     val_ref, dif_ref, conc_ref, prev_ref, phi_ref, own_ref, par_ref, big, small,
-    phi_e, faces, flows, beside, columns, charge, tab_p, tab_m, tab_d, edge_h, edge_l, coef,
+    phi_e, faces, flows, beside, columns, charge, decay_h, decay_l, length_t, tab_d, edges, coef,
     send1, recv1, send_g, recv_g, send2, recv2,
     sig, cols, cols_in, plane_in, conc_in,
     jacc, jmean, jrecv, jsum, jwide, jpiece, jall, jtab, src,
@@ -177,6 +192,20 @@
             row, height, width = places[name, k]
             return big[pl.ds(row, height), pl.ds(0, width)]
         return half(0), half(1)
+
+    def twin(name):
+        row, height, width = places[name, 0]
+        return big[pl.ds(row, height), pl.ds(0, width)]
+
+    def product_twin(name, value):
+        both = twin(name)
+        high, low = split(value)
+        width = value.shape[1]
+        value = jnp.concatenate(
+            [jnp.concatenate([high, high], axis=0), jnp.concatenate([low, jnp.zeros_like(low)], axis=0)], axis=1
+        )
+        found = dot(both, value)
+        return found[:, :width] + found[:, width:]
 
     lane = iota((rows, cy), 1)
     row = iota((rows, cy), 0)
@@ -281,16 +310,18 @@
     tab_d[...] = 1.0 / (lam + small[2:3, 0:cy])
     place = iota((modes, cy), 1).astype(f32)
     power = lambda n: jnp.exp(-theta * n)
-    tab_p[...] = power(place)
-    tab_m[...] = power(cy - 1.0 - place)
+    down = iota((cy, modes), 0).astype(f32)
+    high, low = split(jnp.concatenate([jnp.exp(-theta_row * down), jnp.exp(-theta_row * (cy - 1.0 - down))], axis=1))
+    decay_h[...] = jnp.concatenate([high, high], axis=0)
+    decay_l[...] = low
     scale = 1.0 / (1.0 - power(2.0 * cy + 2.0))
     edge_left = (power(place + 1.0) - power(2.0 * cy + 1.0 - place)) * scale
     edge_right = (power(cy - place) - power(cy + 2.0 + place)) * scale
     for k, edge in enumerate((edge_left, edge_right)):
         high, low = split(edge)
         here = pl.ds(k * modes, modes)
-        edge_h[here, pl.ds(0, cy)] = high
-        edge_l[here, pl.ds(0, cy)] = low
+        edges[here, 0:cy] = high
+        edges[here, cy : 2 * cy] = low
     width1 = cy * nw + 1
     rowp = lambda n: jnp.exp(-theta_row * n)
     front = 1.0 / ((1.0 - rowp(2.0)) * (1.0 - rowp(2.0 * width1)))
@@ -313,6 +344,11 @@
     jacc[...] = jnp.zeros_like(jacc)
     faces[2] = 0.5 * (sigma + jnp.where(top, 0.0, pltpu.roll(sigma, 1, 0)))
     faces[3] = 0.5 * (sigma + jnp.where(bottom, 0.0, pltpu.roll(sigma, rows - 1, 0)))
+
+    loads["big"].wait()
+    length = twin("lt")
+    length = (length[:, :modes].astype(f32) + length[:, modes:].astype(f32)).T
+    length_t[...] = jnp.concatenate([length, length], axis=1)
 
     for copy in halo:
         copy.wait_recv()
@@ -506,19 +542,7 @@
             else:
                 start_species()
 
-    pick_row = iota((8, 2 * cy), 0)
-    pick_lane = iota((8, 2 * cy), 1)
-    pick = jnp.where(
-        ((pick_row == 0) & (pick_lane < cy)) | ((pick_row == 1) & (pick_lane >= cy)), 1.0, 0.0
-    ).astype(bf16)
-    nt = (((1,), (1,)), ((), ()))
-
-    ring_row = iota((LANES, cx * modes), 0)
-    ring_at = iota((LANES, cx * modes), 1)
-    ring_pair = lax.rem((ring_row + 1) // 2, cy // 2)
-    ring_keep = (ring_pair == (ring_at // modes) * nb + lax.rem(ring_at, nb))
-    ring_left = lax.rem(ring_row, 2) == 1
-    loads["big"].wait()
+
     pl.semaphore_wait(known.at[1], 1)
 
     for sweep in range(SWEEPS):
@@ -526,38 +550,40 @@
         residual = charge[...]
         for k in range(6):
             residual = residual - faces[k] * (field - near[k])
-        send1[sweep] = product(table("dt"), residual).reshape(send1.shape[1:])
+        send1[sweep] = product_twin("dt", residual).reshape(send1.shape[1:])
         spread_fast(lambda p: send1.at[sweep, p], recv1.at[sweep], SEM_A + sweep, "chan")
         fill(sweep, 0)
         arrived(recv1.at[sweep], SEM_A + sweep)
-        force = product(table("lt"), recv1[sweep].reshape(modes, cy))
-        high, low = split(jnp.concatenate([force * tab_p[...], force * tab_m[...]], axis=1))
-        moments = lax.dot_general(pick, high, nt, preferred_element_type=f32)
-        moments = moments + lax.dot_general(pick, low, nt, preferred_element_type=f32)
-        send_g[sweep] = moments[0:2]
+        arrival = recv1[sweep].reshape(modes, cy)
+        high, low = split(arrival)
+        decayed = dot(jnp.concatenate([high, low], axis=1), decay_h[...]) + dot(high, decay_l[...])
+        moments = jnp.sum(decayed * length_t[...], axis=0, keepdims=True)
+        send_g[sweep, 0:1, :] = moments[:, :modes]
+        send_g[sweep, 1:2, :] = moments[:, modes:]
         if sweep == 0:
             for k in range(3, far_steps + 1):
                 known_w(k)
         spread_fast(lambda p: send_g.at[sweep], recv_g.at[sweep], SEM_G + sweep, "wide")
+        force = product_twin("lt", arrival)
         width = table("wy")
         inner = product_right(product_right(force, width) * tab_d[...], width)
-        inner = product(table("lb"), inner)
+        inner = product_twin("lb", inner)
         fill(sweep, 1)
         arrived(recv_g.at[sweep], SEM_G + sweep)
         got = recv_g[sweep]
         ends = [jnp.sum(jnp.sum(got * coef[k], axis=0), axis=0, keepdims=True) for k in range(2)]
-        back_h, back_l = table("lb")
-        back = back_h.astype(f32) + back_l.astype(f32)
+        back = twin("lb")
+        back = back[:, :modes].astype(f32) + back[:, modes:].astype(f32)
         high, low = split(jnp.concatenate([back * ends[0], back * ends[1]], axis=1))
-        outer = inner + dot(high, edge_h[...]) + dot(low, edge_h[...]) + dot(high, edge_l[...])
+        outer = dot(high, edges[...])
+        outer = inner + outer[:, :cy] + outer[:, cy:] + dot(low, edges[:, 0:cy])
         span = (cx + 2) * nb
         send2[sweep, :, 0:span, :] = outer.reshape(nc, span, cy)
-        long_ends = [jnp.concatenate([one] * cx, axis=1) for one in ends]
-        high, low = split(jnp.where(ring_keep, jnp.where(ring_left, long_ends[0], long_ends[1]), 0.0))
-        ring_h, ring_l = table("lr")
-        ring = lax.dot_general(ring_h, high, nt, preferred_element_type=f32)
-        ring = ring + lax.dot_general(ring_h, low, nt, preferred_element_type=f32)
-        ring = ring + lax.dot_general(ring_l, high, nt, preferred_element_type=f32)
+        lines = twin("lr")
+        lines = lines[: nc * cx].astype(f32) + lines[nc * cx :].astype(f32)
+        lines = jnp.concatenate([lines[x * nc : (x + 1) * nc] * end for x in range(cx) for end in ends], axis=1)
+        high, low = split(lines)
+        ring = dot(high, twin("lp")) + dot(low, twin("lp"))
         send2[sweep, :, span : span + 1, :] = ring.reshape(nc, 1, cy)
         spread_fast(lambda p: send2.at[sweep, p], recv2.at[sweep], SEM_B + sweep, "chan")
         fill(sweep, 2)
@@ -565,7 +591,7 @@
         phi_e[:, 0:cy] += product(table("db"), recv2[sweep, :, 0:span, :].reshape(nc * span, cy))
         ring = recv2[sweep, :, span : span + 1, :].reshape(nc, cy)
         pieces = [pltpu.roll(ring, cy - 2 * j, 1) if j else ring for j in range(cx * nb)]
-        phi_e[nz : nz + rows, cy : 2 * cy] += product(table("dr"), jnp.concatenate(pieces, axis=0))
+        phi_e[nz : nz + rows, cy : 2 * cy] += product_twin("dr", jnp.concatenate(pieces, axis=0))
 
     field, near = phi_near(None)
     out_phi[...] = field
@@ -645,11 +671,11 @@
             pltpu.VMEM((species, 6, rows, cy), f32),
             pltpu.VMEM((rows, cy), f32),
             pltpu.VMEM((rows, cy), f32),
+            pltpu.VMEM((2 * cy, 2 * modes), bf16),
+            pltpu.VMEM((cy, 2 * modes), bf16),
+            pltpu.VMEM((modes, 2 * modes), f32),
             pltpu.VMEM((modes, cy), f32),
-            pltpu.VMEM((modes, cy), f32),
-            pltpu.VMEM((modes, cy), f32),
-            pltpu.VMEM((2 * modes, cy), bf16),
-            pltpu.VMEM((2 * modes, cy), bf16),
+            pltpu.VMEM((2 * modes, 2 * cy), bf16),
             pltpu.VMEM((2, nw, 2, modes), f32),
             pltpu.VMEM((SWEEPS, nc, cx * nb, cy), f32),
             pltpu.VMEM((SWEEPS, nc, cx * nb, cy), f32),

time: 77.1 us -> 76.2 us (0.988)
  Pallas kernels: 74.9 us -> 74 us
    pallas_call x1, Pallas kernels: 74.9 us -> 74 us  [per_device(): pl.pallas_call(functools.partial(kernel, (nc, nw, cx, nz, cy), places), o...]
where the time goes in v4:
time: 76.2 us; the launch traced here: 76.1 us
  Pallas kernels  74 us (97%)
  local copies, waits for them, and re-layouts  1.42 us (2%)
    pallas_call x1, Pallas kernels, per_device(): pl.pallas_call(functools.partial(kernel, (nc, nw, cx, nz, cy), places), o...  74 us

profile of v4, /device:TPU:1, one launch (start us, length us, event | category | flops | bytes accessed | tf_op | source)
XLA Modules:
  0.0 76.1 jit_solution(8932002929334960629)
XLA Ops:
  0.6 74.0 %step.1 = (f32[1024,128]{1,0:T(8,128)S(1)}, f32[128,128]{1,0:T(8,128)S(1)}) custom-call(s32[8]{0:T(128)} %val_hbm.1, f32[8]{0:T(128)} %dif_hbm.1, f32[1024,128]{1,0:T(8,128)} %bitcast.9, f32[1024,128]{1,0:T(8,128)} %bitcast.10, f32[128,128]{1,0:T(8,128)} %bitcast.11, s32[128,128]{1,0:T(8,128)} %bitcast.12, s32[16,128]{1,0:T(8,128)} %bitcast.13, ...), custom_call_target="tpu_custom_call" | custom-call | tf_op jit(solution)/shard_map/step/pallas_call | solution.py:650
  74.6 0.8 %copy.13 = f32[8,2,64,128]{3,2,1,0:T(8,128)} copy(f32[8,2,64,128]{3,2,1,0:T(8,128)S(1)} %bitcast.7) | data formatting | bytes 1048576
  75.4 0.6 copy.14

commit v5 on v4

--- a/solution.py
+++ b/solution.py
@@ -350,7 +350,7 @@
     length = (length[:, :modes].astype(f32) + length[:, modes:].astype(f32)).T
     length_t[...] = jnp.concatenate([length, length], axis=1)
 
-    for copy in halo:
+    for copy in halo[:2]:
         copy.wait_recv()
     known_w(2)
     wall_xl, wall_xr = me_c == 0, me_c == nc - 1
@@ -374,21 +374,22 @@
             jnp.where(at_last, col_r, pltpu.roll(field, cy - 1, 1)),
         ]
 
-    near = neighbours(
-        sigma, plane_in[0, 0] * keep_xl, plane_in[1, 0] * keep_xr,
-        col_in[:, 1:2] * keep_yl, col_in[:, LEVELS + 1 : LEVELS + 2] * keep_yr, 0,
-    )
-    for k in (0, 1, 4, 5):
-        faces[k] = 0.5 * (sigma + near[k])
-    phi_e[0:nz, 0:cy] = plane_in[0, 1] * keep_xl
+    edge_l, edge_r = col_in[:, 1:2] * keep_yl, col_in[:, LEVELS + 1 : LEVELS + 2] * keep_yr
+    faces[4] = 0.5 * (sigma + jnp.where(at_first, edge_l, pltpu.roll(sigma, 1, 1)))
+    faces[5] = 0.5 * (sigma + jnp.where(at_last, edge_r, pltpu.roll(sigma, cy - 1, 1)))
     phi_e[nz : nz + rows, 0:cy] = phi
-    phi_e[nz + rows : 2 * nz + rows, 0:cy] = plane_in[1, 1] * keep_xr
     phi_e[0:nz, cy : 2 * cy] = jnp.zeros((nz, cy), f32)
     phi_e[nz + rows : 2 * nz + rows, cy : 2 * cy] = jnp.zeros((nz, cy), f32)
     zero = jnp.zeros((rows, cy), f32)
     phi_e[nz : nz + rows, cy : 2 * cy] = jnp.where(
         at_last, col_in[:, 0:1] * keep_yl, jnp.where(at_first, col_in[:, LEVELS : LEVELS + 1] * keep_yr, zero)
     )
+    for copy in halo[2:]:
+        copy.wait_recv()
+    faces[0] = 0.5 * (sigma + jnp.concatenate([plane_in[0, 0] * keep_xl, sigma[: rows - nz]], axis=0))
+    faces[1] = 0.5 * (sigma + jnp.concatenate([sigma[nz:], plane_in[1, 0] * keep_xr], axis=0))
+    phi_e[0:nz, 0:cy] = plane_in[0, 1] * keep_xl
+    phi_e[nz + rows : 2 * nz + rows, 0:cy] = plane_in[1, 1] * keep_xr
 
     def phi_near(beyond):
         field = phi_e[nz : nz + rows, 0:cy]

time: 76.2 us -> 76.2 us (level)
  no operation moved by 1% of the time
where the time goes in v5:
time: 76.2 us; the launch traced here: 76.1 us
  Pallas kernels  74 us (97%)
  local copies, waits for them, and re-layouts  1.42 us (2%)
    pallas_call x1, Pallas kernels, per_device(): pl.pallas_call(functools.partial(kernel, (nc, nw, cx, nz, cy), places), o...  74 us

profile of v5, /device:TPU:1, one launch (start us, length us, event | category | flops | bytes accessed | tf_op | source)
XLA Modules:
  0.0 76.1 jit_solution(548275768853496354)
XLA Ops:
  0.6 74.0 %step.1 = (f32[1024,128]{1,0:T(8,128)S(1)}, f32[128,128]{1,0:T(8,128)S(1)}) custom-call(s32[8]{0:T(128)} %val_hbm.1, f32[8]{0:T(128)} %dif_hbm.1, f32[1024,128]{1,0:T(8,128)} %bitcast.9, f32[1024,128]{1,0:T(8,128)} %bitcast.10, f32[128,128]{1,0:T(8,128)} %bitcast.11, s32[128,128]{1,0:T(8,128)} %bitcast.12, s32[16,128]{1,0:T(8,128)} %bitcast.13, ...), custom_call_target="tpu_custom_call" | custom-call | tf_op jit(solution)/shard_map/step/pallas_call | solution.py:651
  74.6 0.8 %copy.13 = f32[8,2,64,128]{3,2,1,0:T(8,128)} copy(f32[8,2,64,128]{3,2,1,0:T(8,128)S(1)} %bitcast.7) | data formatting | bytes 1048576
  75.4 0.6 copy.14
